TPU v7x, 128 devices: a whole 4x4x4 slice. The times are simulated.
128 devices in a mesh: tm: 8 (over y, core), asset: 16 (over x, z).
Axes of the slice: x: 4, y: 4, z: 4, core: 2. Of those that a mesh axis runs over, the one named last changes fastest.
Arguments:
- features: bfloat16 [16, 20480, 512], P('tm', 'asset'), may hold values from -6 to 6
- w_value: bfloat16 [512, 512], replicated, may hold values from -0.25 to 0.25
- w_gate: bfloat16 [512, 512], replicated, may hold values from -0.25 to 0.25
- cotangent: bfloat16 [16, 20480, 512], P('tm', 'asset'), may hold values from -6 to 6
- local_rows: int32 [320], P('asset'), may hold values from 0 to 9
- local_cols: int32 [320], P('asset'), may hold values from 0 to 9
- local_count: int32 [16], P('asset'), may hold values from 10 to 20, as said below
- local_tiles: bfloat16 [320, 128, 128], P('asset'), may hold values from -0.3125 to 0.3125
- remote_rows: int32 [256], P('asset'), may hold values from 0 to 9
- remote_cols: int32 [256], P('asset'), may hold values from 0 to 9
- remote_live: int32 [256], P('asset'), may hold values from 0 to 1, as said below
- remote_tiles: bfloat16 [256, 128, 128], P('asset'), may hold values from -0.3125 to 0.3125
Outputs:
- output: bfloat16 [16, 20480, 512], P('tm', 'asset')
- grad_features: bfloat16 [16, 20480, 512], P('tm', 'asset')
- grad_value: float32 [512, 512], replicated
- grad_gate: float32 [512, 512], replicated
Inputs may be any that keep to these rules, and one draw needn't show every extreme that they name: `local_count`: used local slots of each index of asset; some index uses all 20 in every draw. `remote_live`: at most one remote tile for each pair of indices of asset, never from an index to itself; in every draw some index holds a tile for every other index, and some index receives a tile from every other index.
All inputs are finite; a program needn't handle non-finite values.
Results may differ from a plain program's by a relative error of at most 0.0057.
Values may be sent and summed in bfloat16 or wider, within the bound.
A program may use at most 128 MiB of HBM per device.

v0:
```python
import jax
import jax.numpy as jnp
from jax import lax
from jax.sharding import PartitionSpec as P


def split_up(array, dim, size):
    shape = array.shape
    blocks = array.reshape(*shape[:dim], size, shape[dim] // size, *shape[dim + 1 :])
    return jnp.moveaxis(blocks, dim, 0)


def edges_of(length, count):
    unit = 8 if length >= 8 * count else 1
    return [length // unit * k // count * unit for k in range(1, count)]


def joined_along(blocks, dim):
    blocks = jnp.moveaxis(blocks, 0, dim)
    shape = blocks.shape
    return blocks.reshape(*shape[:dim], shape[dim] * shape[dim + 1], *shape[dim + 2 :])


def cut_exchange(array, axis, pieces, split_dim, concat_dim):
    blocks = split_up(array, split_dim, lax.axis_size(axis))
    cut = max(range(1, max(2, blocks.ndim - 1)), key=lambda d: blocks.shape[d])
    outs = []
    for slab in jnp.split(blocks, edges_of(blocks.shape[cut], pieces), axis=cut):
        if slab.size:
            outs.append(lax.all_to_all(slab, axis, split_axis=0, concat_axis=0, tiled=True))
    return joined_along(jnp.concatenate(outs, axis=cut), concat_dim)


def one_hot_rows(indices, blocks):
    return (indices[None, :] == jnp.arange(blocks, dtype=jnp.int32)[:, None]).astype(jnp.bfloat16)


def per_device(
    features,
    w_value,
    w_gate,
    cotangent,
    local_rows,
    local_cols,
    local_count,
    local_tiles,
    remote_rows,
    remote_cols,
    remote_live,
    remote_tiles,
):
    steps, assets, width = features.shape
    tile = local_tiles.shape[1]
    blocks = assets // tile
    slots = local_tiles.shape[0]
    flat = features.reshape(-1, width)
    value = jnp.dot(flat, w_value, preferred_element_type=jnp.float32).astype(jnp.bfloat16)
    gate = jax.nn.sigmoid(jnp.dot(flat, w_gate, preferred_element_type=jnp.float32))
    value_blocks = value.reshape(steps, blocks, tile, width)
    live_local = (jnp.arange(slots, dtype=jnp.int32) < local_count[0]).astype(jnp.bfloat16)
    masked_remote = remote_tiles * remote_live.astype(jnp.bfloat16)[:, None, None]
    row_select = one_hot_rows(local_rows, blocks) * live_local[None, :]
    col_select = one_hot_rows(local_cols, blocks) * live_local[None, :]
    in_select = one_hot_rows(remote_rows, blocks)
    out_select = one_hot_rows(remote_cols, blocks)
    sent_blocks = jnp.take(value_blocks, remote_cols, axis=1)
    terms = jnp.einsum(
        "sij,tsjd->tsid", masked_remote, sent_blocks, preferred_element_type=jnp.float32
    ).astype(jnp.bfloat16)
    arrived = cut_exchange(terms, "asset", 2, 1, 1)
    picked = jnp.take(value_blocks, local_cols, axis=1)
    local_terms = jnp.einsum(
        "lij,tljd->tlid", local_tiles, picked, preferred_element_type=jnp.float32
    ).astype(jnp.bfloat16)
    agg_blocks = jnp.einsum(
        "bl,tlid->tbid", row_select, local_terms, preferred_element_type=jnp.float32
    )
    agg_blocks = agg_blocks + jnp.einsum(
        "bs,tsid->tbid", in_select, arrived, preferred_element_type=jnp.float32
    )
    agg = agg_blocks.reshape(-1, width)
    output = (flat.astype(jnp.float32) + gate * agg).astype(jnp.bfloat16)
    grad_out = cotangent.reshape(-1, width).astype(jnp.float32)
    dagg = (grad_out * gate).astype(jnp.bfloat16)
    dgate = (grad_out * agg * gate * (1.0 - gate)).astype(jnp.bfloat16)
    dagg_blocks = dagg.reshape(steps, blocks, tile, width)
    rows_needed = jnp.take(dagg_blocks, remote_rows, axis=1)
    returned = lax.all_to_all(rows_needed, "asset", split_axis=1, concat_axis=1, tiled=True)
    back = jnp.einsum(
        "sji,tsjd->tsid", masked_remote, returned, preferred_element_type=jnp.float32
    ).astype(jnp.bfloat16)
    taken = jnp.take(dagg_blocks, local_rows, axis=1)
    local_back = jnp.einsum(
        "lji,tljd->tlid", local_tiles, taken, preferred_element_type=jnp.float32
    ).astype(jnp.bfloat16)
    grad_blocks = jnp.einsum(
        "bl,tlid->tbid", col_select, local_back, preferred_element_type=jnp.float32
    )
    grad_blocks = grad_blocks + jnp.einsum(
        "bs,tsid->tbid", out_select, back, preferred_element_type=jnp.float32
    )
    dvalue = grad_blocks.reshape(-1, width).astype(jnp.bfloat16)
    grad_features = grad_out + jnp.dot(dvalue, w_value.T, preferred_element_type=jnp.float32)
    grad_features = grad_features + jnp.dot(dgate, w_gate.T, preferred_element_type=jnp.float32)
    partial_value = jnp.dot(flat.T, dvalue, preferred_element_type=jnp.float32)
    partial_gate = jnp.dot(flat.T, dgate, preferred_element_type=jnp.float32)
    total_value, total_gate = lax.psum((partial_value, partial_gate), ("tm", "asset"))
    scale = float(steps * assets * lax.axis_size("tm") * lax.axis_size("asset")) ** (-0.5)
    return (
        output.reshape(steps, assets, width),
        grad_features.astype(jnp.bfloat16).reshape(steps, assets, width),
        total_value * scale,
        total_gate * scale,
    )


def solution(mesh):
    return jax.shard_map(
        per_device,
        mesh=mesh,
        in_specs=(
            P("tm", "asset", None),
            P(),
            P(),
            P("tm", "asset", None),
            P("asset"),
            P("asset"),
            P("asset"),
            P("asset", None, None),
            P("asset"),
            P("asset"),
            P("asset"),
            P("asset", None, None),
        ),
        out_specs=(P("tm", "asset", None), P("tm", "asset", None), P(), P()),
        check_vma=False,
    )
```

profile of v0, /device:TPU:1, one launch (start us, length us, event | category | flops | bytes accessed | tf_op | source)
XLA Modules:
  0.0 365.9 jit_solution(4015320259297418851)
XLA Ops:
  7.2 0.0 copy-start
  7.2 0.7 compare_select_fusion.2
  7.9 0.7 compare_and_fusion.2
  8.6 0.7 convert_element_type.78
  9.2 3.3 convolution_convert_fusion
  12.6 2.8 gather_fusion.1
  15.3 3.7 %convert_bitcast_fusion.3 = bf16[16,2,1,128,512]{4,3,1,0,2:T(8,128)(2,1)S(1)} fusion(bf16[16,2,128,512]{3,2,1,0:T(8,128)(2,1)} %gather_fusion.1, pred[16]{0:T(512)(128)(4,1)S(1)} %compare_and_fusion.2, bf16[16,128,128]{2,1,0:T(8,128)(2,1)} %param.27, bf16[16]{0:T(256)(128)(2,1)S(1)} %convert_element_type.78), kind=kOutput, calls=%fused_computation.40 | convolution fusion | flops 542113792 | bytes 8912944 | tf_op jit(solution)/shard_map/sij,tsjd->tsid/dot_general | solution.py:67
  19.0 2.5 slice_bitcast_fusion.1
  21.5 8.6 %all-to-all-start = ((bf16[16,2,1,64,512]{4,3,1,2,0:T(8,128)(2,1)}), bf16[16,2,1,64,512]{4,3,1,2,0:T(8,128)(2,1)}, u32[]{:S(2)}, u32[]{:S(2)}) async-start(bf16[16,2,1,64,512]{4,3,1,2,0:T(8,128)(2,1)} %get-tuple-element.27), calls=%async_computation | async-start | bytes 4194304 | tf_op jit(solution)/shard_map/all_to_all | solution.py:30
  30.2 4.1 %gather_fusion = bf16[20,2,128,512]{3,2,1,0:T(8,128)(2,1)} fusion(bf16[2,10,128,512]{3,2,1,0:T(8,128)(2,1)S(1)} %bitcast.121, s32[1024]{0:T(1024)S(1)} %pad_clamp_fusion.3), kind=kCustom, calls=%fused_computation.clone | custom fusion | bytes 10485840 | tf_op jit(solution)/shard_map/jit(_take)/gather | solution.py:71
  34.3 24.0 %all-to-all-done = bf16[16,2,1,64,512]{4,3,1,2,0:T(8,128)(2,1)} async-done(((bf16[16,2,1,64,512]{4,3,1,2,0:T(8,128)(2,1)}), bf16[16,2,1,64,512]{4,3,1,2,0:T(8,128)(2,1)}, u32[]{:S(2)}, u32[]{:S(2)}) %all-to-all-start) | async-done | bytes 2097184 | tf_op jit(solution)/shard_map/all_to_all | solution.py:30
  58.4 4.6 %all-to-all-start.1 = ((bf16[16,2,1,64,512]{4,3,1,2,0:T(8,128)(2,1)}), bf16[16,2,1,64,512]{4,3,1,2,0:T(8,128)(2,1)}, u32[]{:S(2)}, u32[]{:S(2)}) async-start(bf16[16,2,1,64,512]{4,3,1,2,0:T(8,128)(2,1)} %get-tuple-element.28), calls=%async_computation.1 | async-start | bytes 4194304 | tf_op jit(solution)/shard_map/all_to_all | solution.py:30
  63.0 6.5 %convert_bitcast_fusion.1 = bf16[2,20,128,512]{2,3,0,1:T(8,128)(2,1)} fusion(bf16[20,2,128,512]{3,2,1,0:T(8,128)(2,1)} %gather_fusion, pred[20]{0:T(512)(128)(4,1)S(1)} %compare_and_fusion.3, bf16[20,128,128]{2,1,0:T(8,128)(2,1)S(1)} %copy-done), kind=kOutput, calls=%fused_computation.25 | convolution fusion | flops 676331520 | bytes 11141140 | tf_op jit(solution)/shard_map/lij,tljd->tlid/dot_general | solution.py:72
  69.5 8.6 %copy.37 = bf16[2,20,128,512]{3,1,2,0:T(8,128)(2,1)} copy(bf16[2,20,128,512]{2,3,0,1:T(8,128)(2,1)} %convert_bitcast_fusion.1) | data formatting | bytes 10485760 | tf_op jit(solution)/shard_map/convert_element_type | solution.py:74
  78.9 7.5 %fusion.51 = f32[2,128,512,10]{2,3,1,0:T(8,128)} fusion(bf16[2,20,128,512]{3,1,2,0:T(8,128)(2,1)} %copy.37, s32[20]{0:T(128)S(1)} %copy-done.11, bf16[20]{0:T(256)(128)(2,1)S(1)} %compare_convert_fusion), kind=kOutput, calls=%fused_computation.70 | convolution fusion | flops 52429200 | bytes 10485880 | tf_op jit(solution)/shard_map/bl,tlid->tbid/dot_general | solution.py:75
  86.4 2.8 copy.40
  89.1 2.8 copy.41
  91.9 4.5 %add_bitcast_fusion = f32[2,10,128,512]{3,1,2,0:T(8,128)S(1)} fusion(f32[2,128,512,10]{2,3,1,0:T(8,128)} %fusion.51, bf16[16,2,1,64,512]{4,0,3,1,2:T(8,128)(2,1)S(1)} %copy.41, bf16[16,2,1,64,512]{4,0,3,1,2:T(8,128)(2,1)S(1)} %copy.40, s32[16]{0:T(128)S(1)} %copy-done.10), kind=kOutput, calls=%fused_computation.5 | convolution fusion | flops 45351072 | bytes 14680128 | tf_op jit(solution)/shard_map/bs,tsid->tbid/dot_general | solution.py:78
  96.4 0.0 copy-start.2
  96.4 0.0 copy-start.7
  96.4 0.0 copy-start.13
  96.4 3.0 copy.42
  99.5 5.5 %fusion.5 = (bf16[2560,512]{1,0:T(8,128)(2,1)}, bf16[2560,512]{1,0:T(8,128)(2,1)}, bf16[2560,512]{1,0:T(8,128)(2,1)S(1)}) fusion(f32[2,10,128,512]{3,2,1,0:T(8,128)S(1)} %copy.42, bf16[2,1280,512]{2,1,0:T(8,128)(2,1)S(1)} %copy-done.2, bf16[2,1280,512]{2,1,0:T(8,128)(2,1)S(1)} %copy-done.13, bf16[2560,512]{1,0:T(8,128)(2,1)S(1)} %bitcast.128, ...), kind=kOutput, calls=%fused_computation.14 | convolution fusion | flops 1361838080 | bytes 21495808 | tf_op jit(solution)/shard_map/dot_general | solution.py:58
  105.0 2.8 gather_fusion.3
  107.7 6.4 %copy.45 = bf16[16,2,128,512]{2,3,1,0:T(8,128)(2,1)} copy(bf16[16,2,128,512]{3,2,1,0:T(8,128)(2,1)} %gather_fusion.3) | data formatting | bytes 8388608 | tf_op jit(solution)/shard_map/jit(_take)/gather | solution.py:87
  114.1 4.6 %select_bitcast_fusion = bf16[2,16,128,512]{2,3,0,1:T(8,128)(2,1)} fusion(bf16[16,2,128,512]{2,3,1,0:T(8,128)(2,1)} %copy.45, pred[16]{0:T(512)(128)(4,1)S(1)} %compare_and_fusion), kind=kLoop, calls=%fused_computation.37 | loop fusion | flops 2097152 | bytes 8388624 | tf_op jit(solution)/shard_map/jit(_take)/select_n | solution.py:87
  118.7 6.4 %all-to-all-start.2 = ((bf16[2,16,128,512]{2,3,0,1:T(8,128)(2,1)}), bf16[2,16,128,512]{2,3,0,1:T(8,128)(2,1)}, u32[]{:S(2)}, u32[]{:S(2)}) async-start(bf16[2,16,128,512]{2,3,0,1:T(8,128)(2,1)} %select_bitcast_fusion), calls=%async_computation.2 | async-start | bytes 8388608 | tf_op jit(solution)/shard_map/all_to_all | solution.py:88
  125.1 0.0 all-reduce.3.cloned.1.call-start
  125.2 4.1 %gather_fusion.2 = bf16[20,2,128,512]{3,2,1,0:T(8,128)(2,1)} fusion(bf16[2,10,128,512]{3,2,1,0:T(8,128)(2,1)S(1)} %bitcast.119, s32[1024]{0:T(1024)S(1)} %pad_clamp_fusion.1), kind=kCustom, calls=%fused_computation.2.clone | custom fusion | bytes 10485840 | tf_op jit(solution)/shard_map/jit(_take)/gather | solution.py:92
  129.3 6.6 %convert_bitcast_fusion = bf16[2,20,128,512]{2,3,0,1:T(8,128)(2,1)} fusion(bf16[20,2,128,512]{3,2,1,0:T(8,128)(2,1)} %gather_fusion.2, pred[20]{0:T(512)(128)(4,1)S(1)} %compare_and_fusion.1, bf16[20,128,128]{2,1,0:T(8,128)(2,1)S(1)} %copy-done), kind=kOutput, calls=%fused_computation.24 | convolution fusion | flops 676331520 | bytes 11141140 | tf_op jit(solution)/shard_map/lji,tljd->tlid/dot_general | solution.py:93
  136.0 8.9 %copy.44 = bf16[2,20,128,512]{3,1,2,0:T(8,128)(2,1)} copy(bf16[2,20,128,512]{2,3,0,1:T(8,128)(2,1)} %convert_bitcast_fusion) | data formatting | bytes 10485760 | tf_op jit(solution)/shard_map/convert_element_type | solution.py:95
  144.8 4.4 %convolution_bitcast_fusion = f32[512,512]{0,1:T(8,128)} fusion(bf16[2560,512]{1,0:T(8,128)(2,1)S(1)} %copy-done.4, bf16[2560,512]{1,0:T(8,128)(2,1)} %bitcast.127), kind=kOutput, calls=%fused_computation.47 | convolution fusion | flops 1342177280 | bytes 6291456 | tf_op jit(solution)/shard_map/dot_general | solution.py:106
  149.2 4.7 %fusion.48 = f32[2,128,512,10]{2,3,1,0:T(8,128)} fusion(bf16[2,20,128,512]{3,1,2,0:T(8,128)(2,1)S(1)} %copy-done.1, s32[20]{0:T(128)S(1)} %copy-done.12, bf16[20]{0:T(256)(128)(2,1)S(1)} %compare_convert_fusion), kind=kOutput, calls=%fused_computation.68 | convolution fusion | flops 52429200 | bytes 10485880 | tf_op jit(solution)/shard_map/bl,tlid->tbid/dot_general | solution.py:96
  154.0 17.7 %all-to-all-done.2 = bf16[2,16,128,512]{2,3,0,1:T(8,128)(2,1)} async-done(((bf16[2,16,128,512]{2,3,0,1:T(8,128)(2,1)}), bf16[2,16,128,512]{2,3,0,1:T(8,128)(2,1)}, u32[]{:S(2)}, u32[]{:S(2)}) %all-to-all-start.2) | async-done | bytes 4194336 | tf_op jit(solution)/shard_map/all_to_all | solution.py:88
  171.6 5.4 %convert_bitcast_fusion.2 = bf16[2,16,128,512]{2,3,0,1:T(8,128)(2,1)} fusion(bf16[2,16,128,512]{2,3,0,1:T(8,128)(2,1)} %all-to-all-done.2, bf16[16,128,128]{2,1,0:T(8,128)(2,1)S(1)} %copy-done.6, bf16[16]{0:T(256)(128)(2,1)S(1)} %convert_element_type.78), kind=kOutput, calls=%fused_computation.39 | convolution fusion | flops 539230208 | bytes 8912928 | tf_op jit(solution)/shard_map/sji,tsjd->tsid/dot_general | solution.py:89
  177.1 7.9 %copy.46 = bf16[2,16,128,512]{3,1,2,0:T(8,128)(2,1)} copy(bf16[2,16,128,512]{2,3,0,1:T(8,128)(2,1)} %convert_bitcast_fusion.2) | data formatting | bytes 8388608 | tf_op jit(solution)/shard_map/convert_element_type | solution.py:91
  185.0 6.2 %fusion.16 = bf16[2,10,128,512]{3,1,2,0:T(8,128)(2,1)S(1)} fusion(f32[2,128,512,10]{2,3,1,0:T(8,128)} %fusion.48, bf16[2,16,128,512]{3,1,2,0:T(8,128)(2,1)} %copy.46, s32[16]{0:T(128)S(1)} %copy-done.9), kind=kOutput, calls=%fused_computation.30 | convolution fusion | flops 44564640 | bytes 12058688 | tf_op jit(solution)/shard_map/bs,tsid->tbid/dot_general | solution.py:99
  191.2 1.5 copy.47
  192.6 0.3 copy-done.14
  192.9 2.5 convolution_bitcast_fusion.1
  195.4 0.0 all-reduce.3.cloned.1.call-update
  195.5 0.0 copy-start.8
  195.5 2.8 fusion.67
  198.4 3.3 fusion.2
  201.7 152.9 %all-reduce.3.cloned.1.call-done = (f32[512,512]{0,1:T(8,128)}, f32[512,512]{0,1:T(8,128)}) async-done(((f32[512,512]{0,1:T(8,128)}, f32[512,512]{0,1:T(8,128)}), (f32[512,512]{0,1:T(8,128)}, f32[512,512]{0,1:T(8,128)})) %all-reduce.3.cloned.1.call-update) | async-done | bytes 2097168 | tf_op jit(solution)/shard_map/psum | solution.py:107
  354.6 1.8 broadcast_multiply_fusion
  356.4 1.3 copy.48
  357.7 1.3 copy.49
  (36 shorter events, 0.1 us)
Async XLA Ops:
  7.2 55.9 %copy-start = (bf16[20,128,128]{2,1,0:T(8,128)(2,1)S(1)}, bf16[20,128,128]{2,1,0:T(8,128)(2,1)}, u32[]{:S(2)}) copy-start(bf16[20,128,128]{2,1,0:T(8,128)(2,1)} %param.23) | copy-start | bytes 1966084
  21.5 8.6 %copy-start.12 = (s32[20]{0:T(128)S(1)}, s32[20]{0:T(128)}, u32[]{:S(2)}) copy-start(s32[20]{0:T(128)} %param.21) | copy-start | bytes 244
  21.5 36.8 %all-to-all-start = ((bf16[16,2,1,64,512]{4,3,1,2,0:T(8,128)(2,1)}), bf16[16,2,1,64,512]{4,3,1,2,0:T(8,128)(2,1)}, u32[]{:S(2)}, u32[]{:S(2)}) async-start(bf16[16,2,1,64,512]{4,3,1,2,0:T(8,128)(2,1)} %get-tuple-element.27), calls=%async_computation | async-start | bytes 4194304 | tf_op jit(solution)/shard_map/all_to_all | solution.py:30
  58.4 30.7 %all-to-all-start.1 = ((bf16[16,2,1,64,512]{4,3,1,2,0:T(8,128)(2,1)}), bf16[16,2,1,64,512]{4,3,1,2,0:T(8,128)(2,1)}, u32[]{:S(2)}, u32[]{:S(2)}) async-start(bf16[16,2,1,64,512]{4,3,1,2,0:T(8,128)(2,1)} %get-tuple-element.28), calls=%async_computation.1 | async-start | bytes 4194304 | tf_op jit(solution)/shard_map/all_to_all | solution.py:30
  69.5 9.3 %copy-start.10 = (s32[16]{0:T(128)S(1)}, s32[16]{0:T(128)}, u32[]{:S(2)}) copy-start(s32[16]{0:T(128)} %param.24) | copy-start | bytes 196
  69.5 9.3 %copy-start.11 = (s32[20]{0:T(128)S(1)}, s32[20]{0:T(128)}, u32[]{:S(2)}) copy-start(s32[20]{0:T(128)} %param.20) | copy-start | bytes 244
  96.4 3.1 copy-start.2
  96.4 3.1 copy-start.7
  96.4 3.1 copy-start.13
  118.7 52.9 %all-to-all-start.2 = ((bf16[2,16,128,512]{2,3,0,1:T(8,128)(2,1)}), bf16[2,16,128,512]{2,3,0,1:T(8,128)(2,1)}, u32[]{:S(2)}, u32[]{:S(2)}) async-start(bf16[2,16,128,512]{2,3,0,1:T(8,128)(2,1)} %select_bitcast_fusion), calls=%async_computation.2 | async-start | bytes 8388608 | tf_op jit(solution)/shard_map/all_to_all | solution.py:88
  125.1 229.5 %all-reduce.3.cloned.1.call-start = ((), (), s32[]{:S(2)}) async-start(), calls=%async_computation.3 | async-start | bytes 4194304 | tf_op jit(solution)/shard_map/psum | solution.py:107
  136.0 8.9 %copy-start.4 = (bf16[2560,512]{1,0:T(8,128)(2,1)S(1)}, bf16[2560,512]{1,0:T(8,128)(2,1)}, u32[]{:S(2)}) copy-start(bf16[2560,512]{1,0:T(8,128)(2,1)} %get-tuple-element.24) | copy-start | bytes 7864324
  144.8 4.4 %copy-start.1 = (bf16[2,20,128,512]{3,1,2,0:T(8,128)(2,1)S(1)}, bf16[2,20,128,512]{3,1,2,0:T(8,128)(2,1)}, u32[]{:S(2)}) copy-start(bf16[2,20,128,512]{3,1,2,0:T(8,128)(2,1)} %copy.44) | copy-start | bytes 15728644
  149.2 22.4 %copy-start.6 = (bf16[16,128,128]{2,1,0:T(8,128)(2,1)S(1)}, bf16[16,128,128]{2,1,0:T(8,128)(2,1)}, u32[]{:S(2)}) copy-start(bf16[16,128,128]{2,1,0:T(8,128)(2,1)} %param.27) | copy-start | bytes 1572868
  177.0 7.9 %copy-start.9 = (s32[16]{0:T(128)S(1)}, s32[16]{0:T(128)}, u32[]{:S(2)}) copy-start(s32[16]{0:T(128)} %param.25) | copy-start | bytes 196
  191.2 1.7 copy-start.14
  195.4 2.9 copy-start.3
  195.5 2.9 copy-start.5
  195.5 2.9 copy-start.8
Sparse Core Ops, SparseCore 0:
  195.6 158.9 all-reduce.2
where the time goes:
time: 367 us; the launch traced here: 366 us
  waiting for transfers between devices  195 us (53%)
  matrix products  67.1 us (18%)
  local copies, waits for them, and re-layouts  61 us (17%)
  starting transfers between devices  19.7 us (5%)
  between operations  15 us (4%)
  other arithmetic  8.48 us (2%)
    psum x1, waiting for transfers between devices, per_device(): lax.psum((partial_value, partial_gate), ('tm', 'asset'))  153 us
    all_to_all x2, waiting for transfers between devices, cut_exchange(): lax.all_to_all(slab, axis, split_axis=0, concat_axis=0, tiled=True)  24.1 us
    all_to_all x1, waiting for transfers between devices, per_device(): lax.all_to_all(rows_needed, 'asset', split_axis=1, concat_axis=1, tiled=T...  17.7 us
    all_to_all x2, starting transfers between devices, cut_exchange(): lax.all_to_all(slab, axis, split_axis=0, concat_axis=0, tiled=True)  13.3 us
    gather x2, local copies, waits for them, and re-layouts, per_device(): rows_needed = jnp.take(dagg_blocks, remote_rows, axis=1)  9.14 us
    convert_element_type x1, local copies, waits for them, and re-layouts, per_device(): local_back = jnp.einsum('lji,tljd->tlid', local_tiles, taken, preferred_e...  8.85 us
    convert_element_type x1, local copies, waits for them, and re-layouts, per_device(): local_terms = jnp.einsum('lij,tljd->tlid', local_tiles, picked, preferred...  8.62 us
    convert_element_type x1, local copies, waits for them, and re-layouts, per_device(): back = jnp.einsum('sji,tsjd->tsid', masked_remote, returned, preferred_el...  7.9 us
  transfers between devices with their start and end apart: 4, of which 3 were waited for; matrix products, arithmetic and copies ran while one was open for 18% of the time, Pallas kernels for 0%

commit v1 on v0

v1 whole, which is shorter than its diff:
```python
import functools

import jax
import jax.numpy as jnp
from jax import lax
from jax.experimental import pallas as pl
from jax.experimental.pallas import tpu as pltpu
from jax.sharding import PartitionSpec as P

MESH = pl.DeviceIdType.MESH
F32 = jnp.float32
BF16 = jnp.bfloat16
NX, NZ, NY, NC = 4, 4, 4, 2
STEPS, BLOCKS, TILE, D = 2, 10, 128, 512
PEERS = NX * NZ - 1
LOC = 20
ZERO = BLOCKS + LOC
ROWS = STEPS * BLOCKS
SCALE = float(16 * 20480) ** -0.5


def offset(k):
    j = k - 3
    pair = j // 2
    odd = j % 2
    near_dx = 1 + 2 * odd
    near_dz = jnp.where(odd == 0, pair, (4 - pair) % 4)
    far_dz = j - 8
    dx = jnp.where(k < 3, 0, jnp.where(k < 11, near_dx, 2))
    dz = jnp.where(k < 3, k + 1, jnp.where(k < 11, near_dz, far_dz))
    return dx, dz


def place():
    asset, tm = lax.axis_index("asset"), lax.axis_index("tm")
    return asset // NZ, asset % NZ, tm // NC, tm % NC


def sent_to(k):
    x, z, _, _ = place()
    dx, dz = offset(k)
    return (x + dx) % NX * NZ + (z + dz) % NZ


def came_from(k):
    x, z, _, _ = place()
    dx, dz = offset(k)
    return (x + NX - dx) % NX * NZ + (z + NZ - dz) % NZ


def chain_tables(rows, cols, count, rrows, rcols, links, heads):
    live = count[0]

    def local_link(src, way):
        def entry(l, _):
            mine = src[l]
            found = jnp.int32(ZERO)
            for m in range(LOC):
                hit = (src[m] == mine) & (m < l) & (m < live)
                found = jnp.where(hit, BLOCKS + m, found)
            links[way, l] = found
            return 0

        lax.fori_loop(0, LOC, entry, 0)

        def head(r, _):
            found = jnp.int32(ZERO)
            for m in range(LOC):
                found = jnp.where((src[m] == r) & (m < live), BLOCKS + m, found)
            heads[way, r] = found
            return 0

        lax.fori_loop(0, BLOCKS, head, 0)

    def remote_link(src, way):
        def entry(k, _):
            mine = src[came_from(k)]
            found = mine
            for m in range(PEERS):
                hit = (src[came_from(m)] == mine) & (m < k)
                found = jnp.where(hit, BLOCKS + m, found)
            links[way, k] = found
            return 0

        lax.fori_loop(0, PEERS, entry, 0)

        def head(r, _):
            found = r
            for m in range(PEERS):
                found = jnp.where(src[came_from(m)] == r, BLOCKS + m, found)
            heads[way, r] = found
            return 0

        lax.fori_loop(0, BLOCKS, head, 0)

    local_link(rows, 0)
    remote_link(rrows, 1)
    local_link(cols, 2)
    remote_link(rcols, 3)


def dot(a, b, ca, cb):
    return lax.dot_general(a, b, (((ca,), (cb,)), ((), ())), preferred_element_type=F32)


def kernel(
    rows, cols, count, rrows, rcols, rlive,
    feat_hbm, cot_hbm, wv_hbm, wg_hbm, lt_hbm, rt_hbm,
    out_hbm, gf_hbm, gv_hbm, gg_hbm,
    feat, cot, wv, wg, lt, rt,
    sf, rf, sb, rb, slots, gate, dagg, gsum, dgate, outs,
    part, core_in, acc, y_in, mine, xz_in, full,
    links, heads,
    load_sem, store_sem, sf_sem, rf_sem, sb_sem, rb_sem,
    core_s, core_r, y_s, y_r, xz_s, xz_r,
):
    x, z, y, c = place()
    asset, tm = lax.axis_index("asset"), lax.axis_index("tm")

    loads = []
    for i, (src, dst) in enumerate(
        ((feat_hbm, feat), (rt_hbm, rt), (wg_hbm, wg), (cot_hbm, cot), (lt_hbm, lt), (wv_hbm, wv))
    ):
        copy = pltpu.make_async_copy(src, dst, load_sem.at[i])
        copy.start()
        loads.append(copy)

    def core_peer():
        return (y * NC + (1 - c), asset)

    def y_peer(dy):
        return ((y + dy) % NY * NC + c, asset)

    barrier = pltpu.get_barrier_semaphore()

    def greet(k, _):
        pl.semaphore_signal(barrier, inc=1, device_id=(tm, sent_to(k)), device_id_type=MESH)
        return 0

    lax.fori_loop(0, PEERS, greet, 0)
    for dy in (1, 2, 3):
        pl.semaphore_signal(barrier, inc=1, device_id=y_peer(dy), device_id_type=MESH)
    pl.semaphore_signal(barrier, inc=1, device_id=core_peer(), device_id_type=MESH)
    pl.semaphore_wait(barrier, PEERS + 4)

    def exchange(k, src, dst, ssem, rsem):
        return pltpu.make_async_remote_copy(
            src_ref=src.at[k], dst_ref=dst.at[k], send_sem=ssem.at[k], recv_sem=rsem.at[k],
            device_id=(tm, sent_to(k)), device_id_type=MESH,
        )

    def masked(peer):
        return (rt[peer].astype(F32) * rlive[peer].astype(F32)).astype(BF16)

    loads[0].wait()
    loads[1].wait()

    def send_term(k, _):
        peer = sent_to(k)
        tile = masked(peer)
        col = rcols[peer]
        for t in range(STEPS):
            sf[k, t] = dot(tile, feat[t * BLOCKS + col], 1, 0).astype(BF16)
        exchange(k, sf, rf, sf_sem, rf_sem).start()
        return 0

    lax.fori_loop(0, PEERS, send_term, 0)

    loads[2].wait()
    loads[3].wait()

    def gate_step(i, _):
        logits = dot(feat[pl.ds(2 * i, 2)].reshape(2 * TILE, D), wg[...], 1, 0)
        g = jax.nn.sigmoid(logits).reshape(2, TILE, D)
        gate[pl.ds(2 * i, 2)] = g
        dagg[pl.ds(2 * i, 2)] = (cot[pl.ds(2 * i, 2)].astype(F32) * g).astype(BF16)
        return 0

    lax.fori_loop(0, ROWS // 2, gate_step, 0)

    def send_back(k, _):
        row = rrows[sent_to(k)]
        for t in range(STEPS):
            sb[k, t] = dagg[t * BLOCKS + row]
        exchange(k, sb, rb, sb_sem, rb_sem).start()
        return 0

    lax.fori_loop(0, PEERS, send_back, 0)

    chain_tables(rows, cols, count, rrows, rcols, links, heads)
    slots[ZERO] = jnp.zeros((STEPS, TILE, D), F32)
    loads[4].wait()

    def local_chain(src, blocks, way, side):
        def entry(l, _):
            tile = lt[l]
            other = src[l]
            for t in range(STEPS):
                slots[BLOCKS + l, t] = slots[links[way, l], t] + dot(tile, blocks[t * BLOCKS + other], side, 0)
            return 0

        lax.fori_loop(0, LOC, entry, 0)

        def base(r, _):
            slots[r] = slots[heads[way, r]]
            return 0

        lax.fori_loop(0, BLOCKS, base, 0)

    local_chain(cols, feat, 0, 1)

    def take_term(k, _):
        exchange(k, sf, rf, sf_sem, rf_sem).wait_recv()
        slots[BLOCKS + k] = slots[links[1, k]] + rf[k].astype(F32)
        return 0

    lax.fori_loop(0, PEERS, take_term, 0)
    loads[5].wait()

    def middle(i, _):
        t, r = i // (BLOCKS // 2), i % (BLOCKS // 2) * 2
        at = pl.ds(2 * i, 2)
        gsum[2 * i] = slots[heads[1, r], t].astype(BF16)
        gsum[2 * i + 1] = slots[heads[1, r + 1], t].astype(BF16)
        agg = dot(gsum[at].reshape(2 * TILE, D), wv[...], 1, 0).reshape(2, TILE, D)
        g = gate[at]
        outs[at] = (feat[at].astype(F32) + g * agg).astype(BF16)
        dgate[at] = (cot[at].astype(F32) * agg * g * (1.0 - g)).astype(BF16)
        return 0

    lax.fori_loop(0, ROWS // 2, middle, 0)
    out_copy = pltpu.make_async_copy(outs, out_hbm, store_sem.at[0])
    out_copy.start()

    part[...] = jnp.zeros_like(part)

    def weight_step(i, _):
        at = pl.ds(4 * i, 4)
        part[0] += dot(gsum[at].reshape(4 * TILE, D), dagg[at].reshape(4 * TILE, D), 0, 0)
        part[1] += dot(feat[at].reshape(4 * TILE, D), dgate[at].reshape(4 * TILE, D), 0, 0)
        return 0

    lax.fori_loop(0, ROWS // 4, weight_step, 0)

    core_copy = pltpu.make_async_remote_copy(
        src_ref=part.at[1 - c], dst_ref=core_in, send_sem=core_s.at[0], recv_sem=core_r.at[0],
        device_id=core_peer(), device_id_type=MESH,
    )
    core_copy.start()

    def pre_step(i, _):
        at = pl.ds(2 * i, 2)
        gate[at] = cot[at].astype(F32) + dot(dgate[at].reshape(2 * TILE, D), wg[...], 1, 1).reshape(2, TILE, D)
        return 0

    lax.fori_loop(0, ROWS // 2, pre_step, 0)

    core_copy.wait_recv()
    acc[...] = part[c] + core_in[...]

    def y_copy(dy):
        return pltpu.make_async_remote_copy(
            src_ref=acc.at[pl.ds((y + dy) % NY * TILE, TILE)], dst_ref=y_in.at[dy - 1],
            send_sem=y_s.at[dy - 1], recv_sem=y_r.at[dy - 1], device_id=y_peer(dy), device_id_type=MESH,
        )

    y_copies = [y_copy(dy) for dy in (1, 3, 2)]
    for copy in y_copies:
        copy.start()

    local_chain(rows, dagg, 2, 0)

    for copy in y_copies:
        copy.wait_recv()
    mine[...] = acc[pl.ds(y * TILE, TILE), :] + y_in[0] + y_in[1] + y_in[2]

    def spread(k):
        return pltpu.make_async_remote_copy(
            src_ref=mine.at[pl.ds(sent_to(k) * 8, 8)], dst_ref=xz_in.at[k],
            send_sem=xz_s.at[k], recv_sem=xz_r.at[k], device_id=(tm, sent_to(k)), device_id_type=MESH,
        )

    def gather(k):
        return pltpu.make_async_remote_copy(
            src_ref=full.at[c, y, asset], dst_ref=full.at[c, y, asset],
            send_sem=xz_s.at[PEERS + k], recv_sem=xz_r.at[PEERS + k], device_id=(tm, sent_to(k)), device_id_type=MESH,
        )

    def each(count, do):
        def step(k, _):
            do(k)
            return 0

        lax.fori_loop(0, count, step, 0)

    def take_back(k):
        exchange(k, sb, rb, sb_sem, rb_sem).wait_recv()
        tile = masked(came_from(k))
        for t in range(STEPS):
            slots[BLOCKS + k, t] = slots[links[3, k], t] + dot(tile, rb[k, t], 0, 0)

    each(PEERS, lambda k: spread(k).start())
    each(8, take_back)
    each(PEERS, lambda k: spread(k).wait_recv())
    total = mine[pl.ds(asset * 8, 8), :]
    for k in range(PEERS):
        total = total + xz_in[k]
    full[c, y, asset] = total * SCALE
    each(PEERS, lambda k: gather(k).start())
    each(PEERS - 8, lambda k: take_back(k + 8))
    each(PEERS, lambda k: gather(k).wait_recv())

    def y_gather(dy):
        return pltpu.make_async_remote_copy(
            src_ref=full.at[c, y], dst_ref=full.at[c, y], send_sem=y_s.at[2 + dy], recv_sem=y_r.at[2 + dy],
            device_id=y_peer(dy), device_id_type=MESH,
        )

    y_gathers = [y_gather(dy) for dy in (1, 3, 2)]
    for copy in y_gathers:
        copy.start()
    out_copy.wait()

    def finish(i, _):
        t, r = i // (BLOCKS // 2), i % (BLOCKS // 2) * 2
        at = pl.ds(2 * i, 2)
        gsum[2 * i] = slots[heads[3, r], t].astype(BF16)
        gsum[2 * i + 1] = slots[heads[3, r + 1], t].astype(BF16)
        grad = gate[at] + dot(gsum[at].reshape(2 * TILE, D), wv[...], 1, 1).reshape(2, TILE, D)
        outs[at] = grad.astype(BF16)
        return 0

    lax.fori_loop(0, ROWS // 2, finish, 0)
    grad_copy = pltpu.make_async_copy(outs, gf_hbm, store_sem.at[1])
    grad_copy.start()

    for copy in y_gathers:
        copy.wait_recv()
    core_gather = pltpu.make_async_remote_copy(
        src_ref=full.at[c], dst_ref=full.at[c], send_sem=core_s.at[1], recv_sem=core_r.at[1],
        device_id=core_peer(), device_id_type=MESH,
    )
    core_gather.start()
    core_gather.wait_recv()
    gv_copy = pltpu.make_async_copy(full.at[0], gv_hbm, store_sem.at[2])
    gg_copy = pltpu.make_async_copy(full.at[1], gg_hbm, store_sem.at[3])
    gv_copy.start()
    gg_copy.start()

    def sent(k):
        exchange(k, sf, rf, sf_sem, rf_sem).wait_send()
        exchange(k, sb, rb, sb_sem, rb_sem).wait_send()
        spread(k).wait_send()
        gather(k).wait_send()

    each(PEERS, sent)
    core_copy.wait_send()
    core_gather.wait_send()
    for copy in y_copies + y_gathers:
        copy.wait_send()
    grad_copy.wait()
    gv_copy.wait()
    gg_copy.wait()


def per_device(
    features, w_value, w_gate, cotangent, local_rows, local_cols, local_count, local_tiles,
    remote_rows, remote_cols, remote_live, remote_tiles,
):
    smem = pl.BlockSpec(memory_space=pltpu.SMEM)
    hbm = pl.BlockSpec(memory_space=pl.ANY)
    dma = pltpu.SemaphoreType.DMA
    blocks = (ROWS, TILE, D)
    exchanged = (PEERS, STEPS, TILE, D)
    out, grad, gv, gg = pl.pallas_call(
        kernel,
        name="relation",
        out_shape=(
            jax.ShapeDtypeStruct(blocks, BF16),
            jax.ShapeDtypeStruct(blocks, BF16),
            jax.ShapeDtypeStruct((NY, NX * NZ, 8, D), F32),
            jax.ShapeDtypeStruct((NY, NX * NZ, 8, D), F32),
        ),
        in_specs=[smem] * 6 + [hbm] * 6,
        out_specs=(hbm,) * 4,
        scratch_shapes=[
            pltpu.VMEM(blocks, BF16),
            pltpu.VMEM(blocks, BF16),
            pltpu.VMEM((D, D), BF16),
            pltpu.VMEM((D, D), BF16),
            pltpu.VMEM((LOC, TILE, TILE), BF16),
            pltpu.VMEM((NX * NZ, TILE, TILE), BF16),
            pltpu.VMEM(exchanged, BF16),
            pltpu.VMEM(exchanged, BF16),
            pltpu.VMEM(exchanged, BF16),
            pltpu.VMEM(exchanged, BF16),
            pltpu.VMEM((ZERO + 1, STEPS, TILE, D), F32),
            pltpu.VMEM(blocks, F32),
            pltpu.VMEM(blocks, BF16),
            pltpu.VMEM(blocks, BF16),
            pltpu.VMEM(blocks, BF16),
            pltpu.VMEM(blocks, BF16),
            pltpu.VMEM((2, D, D), F32),
            pltpu.VMEM((D, D), F32),
            pltpu.VMEM((D, D), F32),
            pltpu.VMEM((NY - 1, TILE, D), F32),
            pltpu.VMEM((TILE, D), F32),
            pltpu.VMEM((PEERS, 8, D), F32),
            pltpu.VMEM((2, NY, NX * NZ, 8, D), F32),
            pltpu.SMEM((4, LOC), jnp.int32),
            pltpu.SMEM((4, BLOCKS), jnp.int32),
            dma((6,)),
            dma((4,)),
            dma((PEERS,)),
            dma((PEERS,)),
            dma((PEERS,)),
            dma((PEERS,)),
            dma((2,)),
            dma((2,)),
            dma((6,)),
            dma((6,)),
            dma((2 * PEERS,)),
            dma((2 * PEERS,)),
        ],
        compiler_params=pltpu.CompilerParams(
            collective_id=0, has_side_effects=True, vmem_limit_bytes=67043328
        ),
    )(
        local_rows, local_cols, local_count, remote_rows, remote_cols, remote_live,
        features.reshape(blocks), cotangent.reshape(blocks), w_value, w_gate, local_tiles, remote_tiles,
    )
    return (
        out.reshape(features.shape),
        grad.reshape(features.shape),
        gv.reshape(D, D),
        gg.reshape(D, D),
    )


def solution(mesh):
    return jax.shard_map(
        per_device,
        mesh=mesh,
        in_specs=(
            P("tm", "asset", None),
            P(),
            P(),
            P("tm", "asset", None),
            P("asset"),
            P("asset"),
            P("asset"),
            P("asset", None, None),
            P("asset"),
            P("asset"),
            P("asset"),
            P("asset", None, None),
        ),
        out_specs=(P("tm", "asset", None), P("tm", "asset", None), P(), P()),
        check_vma=False,
    )
```

time: 367 us -> 159 us (0.43)
  waiting for transfers between devices: 195 us -> 0 us
  Pallas kernels: 0 us -> 150 us
  matrix products: 67.1 us -> 0 us
  local copies, waits for them, and re-layouts: 61 us -> 7.46 us
  starting transfers between devices: 19.7 us -> 0 us
  between operations: 15 us -> 1.3 us
  other arithmetic: 8.48 us -> 0 us
    psum x1 -> x0, waiting for transfers between devices: 153 us -> none  [per_device(): lax.psum((partial_value, partial_gate), ('tm', 'asset'))]
    pallas_call x0 -> x1, Pallas kernels: none -> 150 us  [per_device(): pl.pallas_call(kernel, name='relation', out_shape=(jax.ShapeDtypeStruct(b...]
    dot_general x14 -> x0, matrix products: 67.1 us -> none  [the longest x1 7.47 us: per_device(): jnp.einsum('bl,tlid->tbid', row_select, local_terms, preferred_element_ty...]
    all_to_all x3 -> x0, waiting for transfers between devices: 41.7 us -> none  [the longest x2 24.1 us: cut_exchange(): lax.all_to_all(slab, axis, split_axis=0, concat_axis=0, tiled=True)]
    convert_element_type x4 -> x0, local copies, waits for them, and re-layouts: 26.8 us -> none  [the longest x1 8.85 us: per_device(): local_back = jnp.einsum('lji,tljd->tlid', local_tiles, taken, preferred_e...]
    gather x5 -> x0, local copies, waits for them, and re-layouts: 20.1 us -> none  [the longest x2 9.14 us: per_device(): rows_needed = jnp.take(dagg_blocks, remote_rows, axis=1)]
    all_to_all x3 -> x0, starting transfers between devices: 19.7 us -> none  [the longest x2 13.3 us: cut_exchange(): lax.all_to_all(slab, axis, split_axis=0, concat_axis=0, tiled=True)]
    all_to_all x2 -> x0, local copies, waits for them, and re-layouts: 5.51 us -> none  [cut_exchange(): lax.all_to_all(slab, axis, split_axis=0, concat_axis=0, tiled=True)]
  transfers between devices with their start and end apart: 4 -> 0, of which waited for: 3 -> 0; matrix products, arithmetic and copies ran while one was open for 18% -> 0% of each run, Pallas kernels for 0% -> 0%
where the time goes in v1:
time: 159 us
  Pallas kernels  150 us (94%)
  local copies, waits for them, and re-layouts  7.46 us (5%)
    pallas_call x1, Pallas kernels, per_device(): pl.pallas_call(kernel, name='relation', out_shape=(jax.ShapeDtypeStruct(b...  150 us
    unnamed x10, local copies, waits for them, and re-layouts  7.46 us

profile of v1, /device:TPU:1, one launch (start us, length us, event | category | flops | bytes accessed | tf_op | source)
XLA Modules:
  0.0 158.7 jit_solution(1508587882448711660)
XLA Ops:
  1.3 150.0 %relation.1 = (bf16[20,128,512]{2,1,0:T(8,128)(2,1)}, bf16[20,128,512]{2,1,0:T(8,128)(2,1)}, f32[4,16,8,512]{3,2,1,0:T(8,128)}, f32[4,16,8,512]{3,2,1,0:T(8,128)}) custom-call(s32[20]{0:T(128)} %rows.1, s32[20]{0:T(128)} %cols.1, s32[1]{0:T(128)S(6)} %copy.20.count, s32[16]{0:T(128)} %rrows.1, s32[16]{0:T(128)} %rcols.1, s32[16]{0:T(128)} %rlive.1, ...), custom_call_target="tpu_custom_call" | custom-call | tf_op jit(solution)/shard_map/relation/pallas_call | solution.py:375
  151.3 0.0 copy-start
  151.3 3.6 %copy.21 = bf16[2,1280,512]{2,1,0:T(8,128)(2,1)} copy(bf16[2,1280,512]{2,1,0:T(8,128)(2,1)} %bitcast.9) | data formatting | bytes 5242880
  154.8 0.0 copy-done
  154.8 0.0 copy-start.2
  154.8 0.0 copy-start.1
  154.9 1.5 copy.22
  156.3 0.5 copy-done.2
  156.8 1.0 copy.23
  157.8 0.0 copy-done.1
  157.8 1.0 copy.24
Async XLA Ops:
  151.3 3.6 %copy-start = (bf16[20,128,512]{2,1,0:T(8,128)(2,1)S(1)}, bf16[20,128,512]{2,1,0:T(8,128)(2,1)}, u32[]{:S(2)}) copy-start(bf16[20,128,512]{2,1,0:T(8,128)(2,1)} %get-tuple-element.9) | copy-start | bytes 7864324
  154.8 2.0 %copy-start.2 = (f32[4,16,8,512]{3,2,1,0:T(8,128)S(1)}, f32[4,16,8,512]{3,2,1,0:T(8,128)}, u32[]{:S(2)}) copy-start(f32[4,16,8,512]{3,2,1,0:T(8,128)} %get-tuple-element.10) | copy-start | bytes 3145732
  154.8 2.9 %copy-start.1 = (f32[4,16,8,512]{3,2,1,0:T(8,128)S(1)}, f32[4,16,8,512]{3,2,1,0:T(8,128)}, u32[]{:S(2)}) copy-start(f32[4,16,8,512]{3,2,1,0:T(8,128)} %get-tuple-element.11) | copy-start | bytes 3145732

commit v2 on v1

v2 whole, which is shorter than its diff:
```python
import functools

import jax
import jax.numpy as jnp
from jax import lax
from jax.experimental import pallas as pl
from jax.experimental.pallas import tpu as pltpu
from jax.sharding import PartitionSpec as P

MESH = pl.DeviceIdType.MESH
F32 = jnp.float32
BF16 = jnp.bfloat16
NX, NZ, NY, NC = 4, 4, 4, 2
STEPS, BLOCKS, TILE, D = 2, 10, 128, 512
PEERS = NX * NZ - 1
LOC = 20
ZERO = BLOCKS + LOC
ROWS = STEPS * BLOCKS
WIDE = 5
SCALE = float(16 * 20480) ** -0.5


HOPS = (1, 3, 2)
ORDER = [(s, 0) for s in HOPS] + [(0, j) for j in HOPS] + [(s, j) for s in HOPS for j in HOPS]


def pick(i, values):
    found = values[-1]
    for n, value in enumerate(values[:-1]):
        found = jnp.where(i == n, value, found)
    return found


def place():
    asset, tm = lax.axis_index("asset"), lax.axis_index("tm")
    return asset // NZ, asset % NZ, tm // NC, tm % NC


def at_distance(dx, dz):
    x, z, _, _ = place()
    return (x + dx) % NX * NZ + (z + dz) % NZ


def from_distance(dx, dz):
    return at_distance(NX - dx, NZ - dz)


def turned(h, first, second):
    return jnp.where(h == 0, first, second), jnp.where(h == 0, second, first)


def chain_tables(rows, cols, count, rrows, rcols, links, heads):
    live = count[0]

    def table(keys, way, start):
        for n, key in enumerate(keys):
            found = start(key)
            for m in range(n):
                found = jnp.where(keys[m] == key, BLOCKS + m, found)
            links[way, n] = found
        for r in range(BLOCKS):
            found = start(r)
            for m, key in enumerate(keys):
                found = jnp.where(key == r, BLOCKS + m, found)
            heads[way, r] = found

    for way, src in ((0, rows), (1, cols)):
        table([jnp.where(n < live, src[n], -1) for n in range(LOC)], way, lambda key: ZERO)
    for h in range(STEPS):
        for way, src in ((2, rrows), (4, rcols)):
            table([src[from_distance(*((s, j), (j, s))[h])] for s, j in ORDER], way + h, lambda key: key)


def dot(a, b, ca, cb):
    return lax.dot_general(a, b, (((ca,), (cb,)), ((), ())), preferred_element_type=F32)


def each(first, last, do):
    def step(k, _):
        do(k)
        return 0

    lax.fori_loop(first, last, step, 0)


def kernel(
    rows, cols, count, rrows, rcols, rlive,
    feat_hbm, cot_hbm, wv_hbm, wg_hbm, lt_hbm, rt_hbm,
    outs, gsum, full,
    feat, cot, wv, wg, lt, rt,
    away, over, last, slots, gate, dagg, dgate,
    part, core_in, acc, y_in, mine, xz_in,
    links, heads,
    load_sem, ex_s, ex_r,
    core_s, core_r, y_s, y_r, xz_s, xz_r,
):
    x, z, y, c = place()
    asset, tm = lax.axis_index("asset"), lax.axis_index("tm")

    loads = []
    for i, (src, dst) in enumerate(
        ((feat_hbm, feat), (rt_hbm, rt), (wg_hbm, wg), (cot_hbm, cot), (lt_hbm, lt), (wv_hbm, wv))
    ):
        copy = pltpu.make_async_copy(src, dst, load_sem.at[i])
        copy.start()
        loads.append(copy)

    def core_peer():
        return (y * NC + (1 - c), asset)

    def y_peer(dy):
        return ((y + dy) % NY * NC + c, asset)

    def other(k):
        return (asset + 1 + k) % (NX * NZ)

    barrier = pltpu.get_barrier_semaphore()
    each(0, PEERS, lambda k: pl.semaphore_signal(barrier, inc=1, device_id=(tm, other(k)), device_id_type=MESH))
    for dy in (1, 2, 3):
        pl.semaphore_signal(barrier, inc=1, device_id=y_peer(dy), device_id_type=MESH)
    pl.semaphore_signal(barrier, inc=1, device_id=core_peer(), device_id_type=MESH)

    def first_hop(e, h, d):
        return pltpu.make_async_remote_copy(
            src_ref=away.at[h, d - 1], dst_ref=over.at[e, h, d],
            send_sem=ex_s.at[e, h, d, 0], recv_sem=ex_r.at[e, h, d, 0],
            device_id=(tm, at_distance(*turned(h, d, 0))), device_id_type=MESH,
        )

    def second_hop(e, h, s, j):
        return pltpu.make_async_remote_copy(
            src_ref=over.at[e, h, s, j], dst_ref=last.at[e, h, s, j - 1],
            send_sem=ex_s.at[e, h, s, j], recv_sem=ex_r.at[e, h, s, j],
            device_id=(tm, at_distance(*turned(h, 0, j))), device_id_type=MESH,
        )

    def masked(peer):
        return (rt[peer].astype(F32) * rlive[peer].astype(F32)).astype(BF16)

    def send(e, block, ready):
        def fill(i):
            d, h = pick(i // 2, HOPS), i % 2
            for j in range(4):
                away[h, d - 1, j] = block(h, at_distance(*turned(h, d, j)))

        def go(i):
            first_hop(e, i % 2, pick(i // 2, HOPS)).start()

        def both(i):
            fill(i)
            go(i)

        each(0, 2, fill)
        ready()
        each(0, 2, go)
        each(2, 6, both)

        def own(h):
            for j in (1, 2, 3):
                over[e, h, 0, j] = block(h, at_distance(*turned(h, 0, j)))

        each(0, 2, own)

        def hand(i):
            second_hop(e, i % 2, 0, pick(i // 2, HOPS)).start()

        each(0, 6, hand)

    def relay(e, first, end):
        def step(i):
            s, h = pick(i // 2, HOPS), i % 2
            first_hop(e, h, s).wait_recv()
            for j in (1, 3, 2):
                second_hop(e, h, s, j).start()

        each(first, end, step)

    loads[0].wait()
    loads[1].wait()

    def term(h, peer):
        return dot(masked(peer), feat[h * BLOCKS + rcols[peer]], 1, 0).astype(BF16)

    send(0, term, lambda: pl.semaphore_wait(barrier, PEERS + 4))

    loads[2].wait()
    loads[3].wait()

    def gate_step(i):
        at = pl.ds(WIDE * i, WIDE)
        logits = dot(feat[at].reshape(WIDE * TILE, D), wg[...], 1, 0)
        g = jax.nn.sigmoid(logits).reshape(WIDE, TILE, D)
        gate[at] = g
        dagg[at] = (cot[at].astype(F32) * g).astype(BF16)

    each(0, ROWS // WIDE, gate_step)
    chain_tables(rows, cols, count, rrows, rcols, links, heads)
    slots[ZERO] = jnp.zeros((STEPS, TILE, D), F32)
    loads[4].wait()

    def local_chain(src, blocks, way, side):
        def entry(l):
            tile = lt[l]
            other_block = src[l]
            for t in range(STEPS):
                slots[BLOCKS + l, t] = slots[links[way, l], t] + dot(tile, blocks[t * BLOCKS + other_block], side, 0)

        each(0, LOC, entry)

        def base(r):
            slots[r] = slots[heads[way, r]]

        each(0, BLOCKS, base)

    local_chain(cols, feat, 0, 1)
    relay(0, 0, 6)

    def sent_away(e):
        each(0, 6, lambda i: first_hop(e, i % 2, i // 2 + 1).wait_send())

    sent_away(0)

    def owed(h, peer):
        return dagg[h * BLOCKS + rrows[peer]]

    send(1, owed, lambda: None)

    def take_near(e, add):
        def direct(i):
            s, h = pick(i // 2, HOPS), i % 2
            add(i // 2, h, from_distance(*turned(h, s, 0)), over[e, h, s, 0])

        def handed(i):
            j, h = pick(i // 2, HOPS), i % 2
            second_hop(e, h, 0, j).wait_recv()
            add(3 + i // 2, h, from_distance(*turned(h, 0, j)), last[e, h, 0, j - 1])

        each(0, 6, direct)
        each(0, 6, handed)

    def take_far(e, add):
        def across(i):
            k, h = i // 2, i % 2
            s, j = pick(k // 3, HOPS), pick(k % 3, HOPS)
            second_hop(e, h, s, j).wait_recv()
            add(6 + k, h, from_distance(*turned(h, s, j)), last[e, h, s, j - 1])

        each(0, 18, across)

    def add_term(k, h, peer, block):
        slots[BLOCKS + k, h] = slots[links[2 + h, k], h] + block.astype(F32)

    take_near(0, add_term)
    take_far(0, add_term)
    loads[5].wait()

    def summed(way, i):
        t, r = WIDE * i // BLOCKS, WIDE * i % BLOCKS
        return jnp.concatenate([slots[heads[way + t, r + n], t].astype(BF16) for n in range(WIDE)])

    def middle(i):
        at = pl.ds(WIDE * i, WIDE)
        total = summed(2, i)
        gsum[at] = total.reshape(WIDE, TILE, D)
        agg = dot(total, wv[...], 1, 0).reshape(WIDE, TILE, D)
        g = gate[at]
        outs[at] = (feat[at].astype(F32) + g * agg).astype(BF16)
        dgate[at] = (cot[at].astype(F32) * agg * g * (1.0 - g)).astype(BF16)

    each(0, ROWS // WIDE, middle)
    part[...] = jnp.zeros_like(part)

    def weight_step(i, _):
        at = pl.ds(4 * i, 4)
        part[0] += dot(gsum[at].reshape(4 * TILE, D), dagg[at].reshape(4 * TILE, D), 0, 0)
        part[1] += dot(feat[at].reshape(4 * TILE, D), dgate[at].reshape(4 * TILE, D), 0, 0)
        return 0

    lax.fori_loop(0, ROWS // 4, weight_step, 0)

    core_copy = pltpu.make_async_remote_copy(
        src_ref=part.at[1 - c], dst_ref=core_in, send_sem=core_s.at[0], recv_sem=core_r.at[0],
        device_id=core_peer(), device_id_type=MESH,
    )
    core_copy.start()
    core_copy.wait_recv()
    acc[...] = (part[c] + core_in[...]).astype(BF16)

    def y_copy(dy):
        return pltpu.make_async_remote_copy(
            src_ref=acc.at[pl.ds((y + dy) % NY * TILE, TILE)], dst_ref=y_in.at[dy - 1],
            send_sem=y_s.at[dy - 1], recv_sem=y_r.at[dy - 1], device_id=y_peer(dy), device_id_type=MESH,
        )

    y_copies = [y_copy(dy) for dy in (1, 3, 2)]
    for copy in y_copies:
        copy.start()

    local_chain(rows, dagg, 1, 0)
    own_rows = pl.ds(y * TILE, TILE)
    mine[...] = part[c, own_rows, :] + core_in[own_rows, :]

    for copy in y_copies:
        copy.wait_recv()
    mine[...] += y_in[0].astype(F32) + y_in[1].astype(F32) + y_in[2].astype(F32)

    def spread(k):
        return pltpu.make_async_remote_copy(
            src_ref=mine.at[pl.ds(other(k) * 8, 8)], dst_ref=xz_in.at[k],
            send_sem=xz_s.at[k], recv_sem=xz_r.at[k], device_id=(tm, other(k)), device_id_type=MESH,
        )

    def gather(k):
        return pltpu.make_async_remote_copy(
            src_ref=full.at[c, y, asset], dst_ref=full.at[c, y, asset],
            send_sem=xz_s.at[PEERS + k], recv_sem=xz_r.at[PEERS + k], device_id=(tm, other(k)), device_id_type=MESH,
        )

    each(0, PEERS, lambda k: spread(k).start())
    relay(1, 0, 4)

    def pre_step(i):
        at = pl.ds(WIDE * i, WIDE)
        gate[at] = cot[at].astype(F32) + dot(dgate[at].reshape(WIDE * TILE, D), wg[...], 1, 1).reshape(WIDE, TILE, D)

    each(0, ROWS // WIDE, pre_step)

    each(0, PEERS, lambda k: spread(k).wait_recv())
    total = mine[pl.ds(asset * 8, 8), :]
    for k in range(PEERS):
        total = total + xz_in[k]
    full[c, y, asset] = (total * SCALE).astype(BF16)
    each(0, PEERS, lambda k: gather(k).start())

    def add_back(k, h, peer, block):
        slots[BLOCKS + k, h] = slots[links[4 + h, k], h] + dot(masked(peer), block, 0, 0)

    relay(1, 4, 6)
    take_near(1, add_back)
    each(0, PEERS, lambda k: gather(k).wait_recv())

    def y_gather(dy):
        return pltpu.make_async_remote_copy(
            src_ref=full.at[c, y], dst_ref=full.at[c, y], send_sem=y_s.at[2 + dy], recv_sem=y_r.at[2 + dy],
            device_id=y_peer(dy), device_id_type=MESH,
        )

    y_gathers = [y_gather(dy) for dy in (1, 3, 2)]
    for copy in y_gathers:
        copy.start()
    take_far(1, add_back)
    for copy in y_gathers:
        copy.wait_recv()
    core_gather = pltpu.make_async_remote_copy(
        src_ref=full.at[c], dst_ref=full.at[c], send_sem=core_s.at[1], recv_sem=core_r.at[1],
        device_id=core_peer(), device_id_type=MESH,
    )
    core_gather.start()

    def finish(i):
        at = pl.ds(WIDE * i, WIDE)
        gsum[at] = (gate[at] + dot(summed(4, i), wv[...], 1, 1).reshape(WIDE, TILE, D)).astype(BF16)

    each(0, ROWS // WIDE, finish)
    core_gather.wait_recv()
    sent_away(1)

    def handed(i):
        for e in range(2):
            for j in (1, 2, 3):
                second_hop(e, i % 2, i // 2, j).wait_send()

    each(0, 8, handed)

    def sent(k):
        spread(k).wait_send()
        gather(k).wait_send()

    each(0, PEERS, sent)
    core_copy.wait_send()
    core_gather.wait_send()
    for copy in y_copies + y_gathers:
        copy.wait_send()


def emit(outs, gsum, full, out_hbm, gf_hbm, gv_hbm, gg_hbm, wide, sem):
    copies = [pltpu.make_async_copy(outs, out_hbm, sem.at[0]), pltpu.make_async_copy(gsum, gf_hbm, sem.at[1])]
    for copy in copies:
        copy.start()
    for i, dst in enumerate((gv_hbm, gg_hbm)):
        wide[i] = full[i].astype(F32)
        copies.append(pltpu.make_async_copy(wide.at[i], dst, sem.at[2 + i]))
        copies[-1].start()
    for copy in copies:
        copy.wait()


def per_device(
    features, w_value, w_gate, cotangent, local_rows, local_cols, local_count, local_tiles,
    remote_rows, remote_cols, remote_live, remote_tiles,
):
    smem = pl.BlockSpec(memory_space=pltpu.SMEM)
    hbm = pl.BlockSpec(memory_space=pl.ANY)
    vmem = pl.BlockSpec(memory_space=pltpu.VMEM)
    dma = pltpu.SemaphoreType.DMA
    blocks = (ROWS, TILE, D)
    reduced = (2, NY, NX * NZ, 8, D)
    held = pl.pallas_call(
        kernel,
        name="relation",
        out_shape=(pltpu.VMEM(blocks, BF16), pltpu.VMEM(blocks, BF16), pltpu.VMEM(reduced, BF16)),
        in_specs=[smem] * 6 + [hbm] * 6,
        out_specs=(vmem,) * 3,
        scratch_shapes=[
            pltpu.VMEM(blocks, BF16),
            pltpu.VMEM(blocks, BF16),
            pltpu.VMEM((D, D), BF16),
            pltpu.VMEM((D, D), BF16),
            pltpu.VMEM((LOC, TILE, TILE), BF16),
            pltpu.VMEM((NX * NZ, TILE, TILE), BF16),
            pltpu.VMEM((2, 3, 4, TILE, D), BF16),
            pltpu.VMEM((2, 2, 4, 4, TILE, D), BF16),
            pltpu.VMEM((2, 2, 4, 3, TILE, D), BF16),
            pltpu.VMEM((ZERO + 1, STEPS, TILE, D), F32),
            pltpu.VMEM(blocks, F32),
            pltpu.VMEM(blocks, BF16),
            pltpu.VMEM(blocks, BF16),
            pltpu.VMEM((2, D, D), F32),
            pltpu.VMEM((D, D), F32),
            pltpu.VMEM((D, D), BF16),
            pltpu.VMEM((NY - 1, TILE, D), BF16),
            pltpu.VMEM((TILE, D), F32),
            pltpu.VMEM((PEERS, 8, D), F32),
            pltpu.SMEM((6, LOC), jnp.int32),
            pltpu.SMEM((6, BLOCKS), jnp.int32),
            dma((6,)),
            dma((2, 2, 4, 4)),
            dma((2, 2, 4, 4)),
            dma((2,)),
            dma((2,)),
            dma((6,)),
            dma((6,)),
            dma((2 * PEERS,)),
            dma((2 * PEERS,)),
        ],
        compiler_params=pltpu.CompilerParams(
            collective_id=0, has_side_effects=True, vmem_limit_bytes=57 << 20
        ),
    )(
        local_rows, local_cols, local_count, remote_rows, remote_cols, remote_live,
        features.reshape(blocks), cotangent.reshape(blocks), w_value, w_gate, local_tiles, remote_tiles,
    )
    wide = jax.ShapeDtypeStruct(reduced[1:], F32)
    out, grad, gv, gg = pl.pallas_call(
        emit,
        name="emit",
        out_shape=(jax.ShapeDtypeStruct(blocks, BF16), jax.ShapeDtypeStruct(blocks, BF16), wide, wide),
        in_specs=[vmem] * 3,
        out_specs=(hbm,) * 4,
        scratch_shapes=[pltpu.VMEM(reduced, F32), dma((4,))],
        compiler_params=pltpu.CompilerParams(vmem_limit_bytes=16 << 20),
    )(*[pltpu.with_memory_space_constraint(a, pltpu.MemorySpace.VMEM) for a in held])
    return (
        out.reshape(features.shape),
        grad.reshape(features.shape),
        gv.reshape(D, D),
        gg.reshape(D, D),
    )


def solution(mesh):
    return jax.shard_map(
        per_device,
        mesh=mesh,
        in_specs=(
            P("tm", "asset", None),
            P(),
            P(),
            P("tm", "asset", None),
            P("asset"),
            P("asset"),
            P("asset"),
            P("asset", None, None),
            P("asset"),
            P("asset"),
            P("asset"),
            P("asset", None, None),
        ),
        out_specs=(P("tm", "asset", None), P("tm", "asset", None), P(), P()),
        check_vma=False,
    )
```

time: 159 us -> 117 us (0.74)
  Pallas kernels: 150 us -> 115 us
  local copies, waits for them, and re-layouts: 7.46 us -> 0 us
    pallas_call x1 -> x2, Pallas kernels: 150 us -> 115 us  [the longest x1 112 us: per_device(): pl.pallas_call(kernel, name='relation', out_shape=(pltpu.VMEM(blocks, BF1...]
    unnamed x10 -> x0, local copies, waits for them, and re-layouts: 7.46 us -> none
where the time goes in v2:
time: 117 us
  Pallas kernels  115 us (98%)
  between operations  1.29 us (1%)
    pallas_call x1, Pallas kernels, per_device(): pl.pallas_call(kernel, name='relation', out_shape=(pltpu.VMEM(blocks, BF1...  112 us
    pallas_call x1, Pallas kernels, per_device(): pl.pallas_call(emit, name='emit', out_shape=(jax.ShapeDtypeStruct(blocks,...  3.05 us

profile of v2, /device:TPU:1, one launch (start us, length us, event | category | flops | bytes accessed | tf_op | source)
XLA Modules:
  0.0 116.8 jit_solution(10077812551759831370)
XLA Ops:
  1.3 112.4 %relation.1 = (bf16[20,128,512]{2,1,0:T(8,128)(2,1)S(1)}, bf16[20,128,512]{2,1,0:T(8,128)(2,1)S(1)}, bf16[2,4,16,8,512]{4,3,2,1,0:T(8,128)(2,1)S(1)}) custom-call(s32[20]{0:T(128)} %rows.1, s32[20]{0:T(128)} %cols.1, s32[1]{0:T(128)S(6)} %copy.16.count, s32[16]{0:T(128)} %rrows.1, s32[16]{0:T(128)} %rcols.1, s32[16]{0:T(128)} %rlive.1, ...), custom_call_target="tpu_custom_call" | custom-call | tf_op jit(solution)/shard_map/relation/pallas_call | solution.py:408
  113.7 3.0 %emit.1 = (bf16[20,128,512]{2,1,0:T(8,128)(2,1)}, bf16[20,128,512]{2,1,0:T(8,128)(2,1)}, f32[4,16,8,512]{3,2,1,0:T(8,128)}, f32[4,16,8,512]{3,2,1,0:T(8,128)}) custom-call(bf16[20,128,512]{2,1,0:T(8,128)(2,1)S(1)} %get-tuple-element.11.outs, bf16[20,128,512]{2,1,0:T(8,128)(2,1)S(1)} %get-tuple-element.12.gsum, ...), custom_call_target="tpu_custom_call" | custom-call | tf_op jit(solution)/shard_map/emit/pallas_call | solution.py:454

commit v3 on v2

v3 whole, which is shorter than its diff:
```python
import functools

import jax
import jax.numpy as jnp
from jax import lax
from jax.experimental import pallas as pl
from jax.experimental.pallas import tpu as pltpu
from jax.sharding import PartitionSpec as P

MESH = pl.DeviceIdType.MESH
F32 = jnp.float32
BF16 = jnp.bfloat16
NX, NZ, NY, NC = 4, 4, 4, 2
STEPS, BLOCKS, TILE, D = 2, 10, 128, 512
PEERS = NX * NZ - 1
LOC = 20
ZERO = BLOCKS + LOC
ROWS = STEPS * BLOCKS
WIDE = 5
GROUP = 5
SCALE = float(16 * 20480) ** -0.5


HOPS = (1, 3, 2)
ORDER = [(s, 0) for s in HOPS] + [(0, j) for j in HOPS] + [(s, j) for s in HOPS for j in HOPS]


def pick(i, values):
    found = values[-1]
    for n, value in enumerate(values[:-1]):
        found = jnp.where(i == n, value, found)
    return found


def place():
    asset, tm = lax.axis_index("asset"), lax.axis_index("tm")
    return asset // NZ, asset % NZ, tm // NC, tm % NC


def at_distance(dx, dz):
    x, z, _, _ = place()
    return (x + dx) % NX * NZ + (z + dz) % NZ


def from_distance(dx, dz):
    return at_distance(NX - dx, NZ - dz)


def turned(h, first, second):
    return jnp.where(h == 0, first, second), jnp.where(h == 0, second, first)


def chain_tables(rows, cols, count, rrows, rcols, links, heads):
    live = count[0]

    def table(keys, way, start):
        for n, key in enumerate(keys):
            found = start(key)
            for m in range(n):
                found = jnp.where(keys[m] == key, BLOCKS + m, found)
            links[way, n] = found
        for r in range(BLOCKS):
            found = start(r)
            for m, key in enumerate(keys):
                found = jnp.where(key == r, BLOCKS + m, found)
            heads[way, r] = found

    for way, src in ((0, rows), (1, cols)):
        table([jnp.where(n < live, src[n], -1) for n in range(LOC)], way, lambda key: ZERO)
    for h in range(STEPS):
        for way, src in ((2, rrows), (4, rcols)):
            table([src[from_distance(*((s, j), (j, s))[h])] for s, j in ORDER], way + h, lambda key: key)


def dot(a, b, ca, cb):
    return lax.dot_general(a, b, (((ca,), (cb,)), ((), ())), preferred_element_type=F32)


def each(first, last, do):
    def step(k, _):
        do(k)
        return 0

    lax.fori_loop(first, last, step, 0)


def kernel(
    count, rows_hbm, cols_hbm, rrows_hbm, rcols_hbm, rlive_hbm,
    feat_hbm, cot_hbm, wv_hbm, wg_hbm, lt_hbm, rt_hbm,
    outs, gsum, gate, full, wv,
    rows, cols, rrows, rcols, rlive,
    feat, cot, wg, lt, rt,
    away, over, last, slots, dagg, dgate,
    part, core_in, acc, y_in, mine, mine_out, xz_in,
    links, heads,
    load_sem, ex_s, first_r, last_r,
    core_s, core_r, y_s, y_r, xz_s, xz_r,
):
    x, z, y, c = place()
    asset, tm = lax.axis_index("asset"), lax.axis_index("tm")

    loads = []
    for i, (src, dst) in enumerate(
        (
            (rcols_hbm, rcols),
            (rlive_hbm, rlive),
            (feat_hbm, feat),
            (rt_hbm, rt),
            (wg_hbm, wg),
            (cot_hbm, cot),
            (rows_hbm, rows),
            (cols_hbm, cols),
            (rrows_hbm, rrows),
            (lt_hbm, lt),
            (wv_hbm, wv),
        )
    ):
        copy = pltpu.make_async_copy(src, dst, load_sem.at[i])
        copy.start()
        loads.append(copy)

    def core_peer():
        return (y * NC + (1 - c), asset)

    def y_peer(dy):
        return ((y + dy) % NY * NC + c, asset)

    def other(k):
        return (asset + 1 + k) % (NX * NZ)

    barrier = pltpu.get_barrier_semaphore()
    each(0, PEERS, lambda k: pl.semaphore_signal(barrier, inc=1, device_id=(tm, other(k)), device_id_type=MESH))
    for dy in (1, 2, 3):
        pl.semaphore_signal(barrier, inc=1, device_id=y_peer(dy), device_id_type=MESH)
    pl.semaphore_signal(barrier, inc=1, device_id=core_peer(), device_id_type=MESH)

    def first_hop(e, h, d):
        return pltpu.make_async_remote_copy(
            src_ref=away.at[h, d - 1], dst_ref=over.at[e, h, d],
            send_sem=ex_s.at[e, 0], recv_sem=first_r.at[e, h, d - 1],
            device_id=(tm, at_distance(*turned(h, d, 0))), device_id_type=MESH,
        )

    def second_hop(e, h, s, j):
        return pltpu.make_async_remote_copy(
            src_ref=over.at[e, h, s, j], dst_ref=last.at[e, h, s, j - 1],
            send_sem=ex_s.at[e, 1], recv_sem=last_r.at[e, h, s],
            device_id=(tm, at_distance(*turned(h, 0, j))), device_id_type=MESH,
        )

    def masked(peer):
        return (rt[peer].astype(F32) * rlive[peer].astype(F32)).astype(BF16)

    def all_of(src, dst, ssem, rsem):
        return pltpu.make_async_remote_copy(
            src_ref=src, dst_ref=dst, send_sem=ssem, recv_sem=rsem, device_id=core_peer(), device_id_type=MESH
        )

    def arrived(e, h, s):
        all_of(last.at[e, h, s], last.at[e, h, s], ex_s.at[e, 1], last_r.at[e, h, s]).wait_recv()

    def send(e, block, ready):
        def fill(i):
            d, h = pick(i // 2, HOPS), i % 2
            for j in range(4):
                away[h, d - 1, j] = block(h, at_distance(*turned(h, d, j)))

        def go(i):
            first_hop(e, i % 2, pick(i // 2, HOPS)).start()

        def both(i):
            fill(i)
            go(i)

        fill(0)
        ready()
        go(0)
        each(1, 6, both)

        def own(h):
            for j in (1, 2, 3):
                over[e, h, 0, j] = block(h, at_distance(*turned(h, 0, j)))

        each(0, 2, own)

    def hand(e):
        def step(i):
            second_hop(e, i % 2, 0, pick(i // 2, HOPS)).start()

        each(0, 6, step)

    def relay(e, first, end):
        def step(i):
            s, h = pick(i // 2, HOPS), i % 2
            first_hop(e, h, s).wait_recv()
            for j in (1, 3, 2):
                second_hop(e, h, s, j).start()

        each(first, end, step)

    for copy in loads[:4]:
        copy.wait()

    def term(h, peer):
        return dot(masked(peer), feat[h * BLOCKS + rcols[peer]], 1, 0).astype(BF16)

    send(0, term, lambda: pl.semaphore_wait(barrier, PEERS + 4))
    hand(0)

    loads[4].wait()
    loads[5].wait()

    def gate_step(i):
        at = pl.ds(WIDE * i, WIDE)
        logits = dot(feat[at].reshape(WIDE * TILE, D), wg[...], 1, 0)
        g = jax.nn.sigmoid(logits).reshape(WIDE, TILE, D)
        gate[at] = g
        dagg[at] = (cot[at].astype(F32) * g).astype(BF16)

    each(0, ROWS // WIDE, gate_step)
    for copy in loads[6:10]:
        copy.wait()
    chain_tables(rows, cols, count, rrows, rcols, links, heads)
    slots[ZERO] = jnp.zeros((STEPS, TILE, D), F32)

    def local_chain(src, blocks, way, side):
        def entry(l):
            tile = lt[l]
            other_block = src[l]
            for t in range(STEPS):
                slots[BLOCKS + l, t] = slots[links[way, l], t] + dot(tile, blocks[t * BLOCKS + other_block], side, 0)

        each(0, LOC, entry)

        def base(r):
            slots[r] = slots[heads[way, r]]

        each(0, BLOCKS, base)

    local_chain(cols, feat, 0, 1)
    relay(0, 0, 6)

    def sent_away(e):
        all_of(away, away, ex_s.at[e, 0], first_r.at[e, 0, 0]).wait_send()

    sent_away(0)

    def owed(h, peer):
        return dagg[h * BLOCKS + rrows[peer]]

    send(1, owed, lambda: None)

    def take_near(e, add):
        def direct(i):
            s, h = pick(i // 2, HOPS), i % 2
            add(i // 2, h, from_distance(*turned(h, s, 0)), over[e, h, s, 0])

        def handed(i):
            j, h = pick(i // 2, HOPS), i % 2
            add(3 + i // 2, h, from_distance(*turned(h, 0, j)), last[e, h, 0, j - 1])

        each(0, 6, direct)
        each(0, 2, lambda h: arrived(e, h, 0))
        each(0, 6, handed)

    def take_far(e, first, end, add):
        def across(i):
            n, h = i // 2, i % 2
            s = pick(n, HOPS)
            arrived(e, h, s)
            for m, j in enumerate(HOPS):
                add(6 + 3 * n + m, h, from_distance(*turned(h, s, j)), last[e, h, s, j - 1])

        each(first, end, across)

    def add_term(k, h, peer, block):
        slots[BLOCKS + k, h] = slots[links[2 + h, k], h] + block.astype(F32)

    take_near(0, add_term)
    take_far(0, 0, 6, add_term)
    loads[10].wait()

    def summed(way, i):
        t, r = WIDE * i // BLOCKS, WIDE * i % BLOCKS
        return jnp.concatenate([slots[heads[way + t, r + n], t] for n in range(WIDE)])

    def middle(i):
        at = pl.ds(WIDE * i, WIDE)
        total = summed(2, i)
        high = total.astype(BF16)
        low = (total - high.astype(F32)).astype(BF16)
        gsum[at] = high.reshape(WIDE, TILE, D)
        agg = (dot(high, wv[...], 1, 0) + dot(low, wv[...], 1, 0)).reshape(WIDE, TILE, D)
        g = gate[at]
        outs[at] = (feat[at].astype(F32) + g * agg).astype(BF16)
        dgate[at] = (cot[at].astype(F32) * agg * g * (1.0 - g)).astype(BF16)

    each(0, ROWS // WIDE, middle)
    def weight(n, left, right):
        def product(i):
            at = pl.ds(BLOCKS * i, BLOCKS)
            return dot(left[at].reshape(BLOCKS * TILE, D), right[at].reshape(BLOCKS * TILE, D), 0, 0)

        part[n] = product(0)
        part[n] += product(1)

    core_copy = pltpu.make_async_remote_copy(
        src_ref=part.at[1 - c], dst_ref=core_in, send_sem=core_s.at[0], recv_sem=core_r.at[0],
        device_id=core_peer(), device_id_type=MESH,
    )
    weight(0, gsum, dagg)

    @pl.when(c == 1)
    def _():
        core_copy.start()

    weight(1, feat, dgate)

    @pl.when(c == 0)
    def _():
        core_copy.start()

    core_copy.wait_recv()
    acc[...] = (part[c] + core_in[...]).astype(BF16)

    def y_copy(dy):
        return pltpu.make_async_remote_copy(
            src_ref=acc.at[pl.ds((y + dy) % NY * TILE, TILE)], dst_ref=y_in.at[dy - 1],
            send_sem=y_s.at[0], recv_sem=y_r.at[0], device_id=y_peer(dy), device_id_type=MESH,
        )

    y_copies = [y_copy(dy) for dy in (1, 3, 2)]
    for copy in y_copies:
        copy.start()

    local_chain(rows, dagg, 1, 0)
    own_rows = pl.ds(y * TILE, TILE)
    mine[...] = part[c, own_rows, :] + core_in[own_rows, :]

    y_all = all_of(y_in, y_in, y_s.at[0], y_r.at[0])
    y_all.wait_recv()
    mine[...] += y_in[0].astype(F32) + y_in[1].astype(F32) + y_in[2].astype(F32)
    mine_out[...] = mine[...].reshape(NX * NZ, 8, D).astype(BF16)

    def spread(k):
        return pltpu.make_async_remote_copy(
            src_ref=mine_out.at[other(k)], dst_ref=xz_in.at[k],
            send_sem=xz_s.at[0], recv_sem=xz_r.at[0], device_id=(tm, other(k)), device_id_type=MESH,
        )

    def gather(k):
        return pltpu.make_async_remote_copy(
            src_ref=full.at[c, y, asset], dst_ref=full.at[c, y, asset],
            send_sem=xz_s.at[1], recv_sem=xz_r.at[1 + k // GROUP], device_id=(tm, other(k)), device_id_type=MESH,
        )

    each(0, PEERS, lambda k: spread(k).start())
    hand(1)
    relay(1, 0, 2)

    def pre_step(i):
        at = pl.ds(WIDE * i, WIDE)
        gate[at] = cot[at].astype(F32) + dot(dgate[at].reshape(WIDE * TILE, D), wg[...], 1, 1).reshape(WIDE, TILE, D)

    each(0, ROWS // WIDE, pre_step)

    spread_all = all_of(xz_in, xz_in, xz_s.at[0], xz_r.at[0])
    spread_all.wait_recv()
    total = mine[pl.ds(asset * 8, 8), :]
    for k in range(PEERS):
        total = total + xz_in[k].astype(F32)
    full[c, y, asset] = (total * SCALE).astype(BF16)
    each(0, PEERS, lambda k: gather(k).start())

    def add_back(k, h, peer, block):
        slots[BLOCKS + k, h] = slots[links[4 + h, k], h] + dot(masked(peer), block, 0, 0)

    relay(1, 2, 6)
    take_near(1, add_back)

    def hand_y(k, dy):
        piece = full.at[c, y, (asset + NX * NZ - 1 - k) % (NX * NZ)]
        return pltpu.make_async_remote_copy(
            src_ref=piece, dst_ref=piece, send_sem=y_s.at[1], recv_sem=y_r.at[1],
            device_id=y_peer(dy), device_id_type=MESH,
        )

    some = full.at[c, y, pl.ds(0, GROUP)]

    def pass_on(g):
        all_of(some, some, xz_s.at[1], xz_r.at[1 + g]).wait_recv()
        for k in range(GROUP):
            for dy in (1, 3, 2):
                hand_y(g * GROUP + k, dy).start()

    for dy in (1, 3, 2):
        hand_y(PEERS, dy).start()
    each(0, PEERS // GROUP, pass_on)
    take_far(1, 0, 4, add_back)
    most = full.at[c, pl.ds(0, NY - 1)]
    hand_all = all_of(most, most, y_s.at[1], y_r.at[1])
    hand_all.wait_recv()
    core_gather = pltpu.make_async_remote_copy(
        src_ref=full.at[c], dst_ref=full.at[c], send_sem=core_s.at[1], recv_sem=core_r.at[1],
        device_id=core_peer(), device_id_type=MESH,
    )
    core_gather.start()
    take_far(1, 4, 6, add_back)

    def settle(i):
        gsum[pl.ds(WIDE * i, WIDE)] = summed(4, i).astype(BF16).reshape(WIDE, TILE, D)

    each(0, ROWS // WIDE, settle)
    sent_away(1)
    for e in range(2):
        all_of(last.at[e], last.at[e], ex_s.at[e, 1], last_r.at[e, 0, 0]).wait_send()
    core_copy.wait_send()
    y_all.wait_send()
    spread_all.wait_send()
    pieces = full.at[c, y, pl.ds(0, PEERS)]
    all_of(pieces, pieces, xz_s.at[1], xz_r.at[1]).wait_send()
    hand_all.wait_send()
    core_gather.wait()


def emit(outs, dvalue, rest, full, wv, out_hbm, gf_hbm, gv_hbm, gg_hbm, grads, wide, sem):
    copies = [pltpu.make_async_copy(outs, out_hbm, sem.at[0])]
    copies[0].start()
    for i, dst in enumerate((gv_hbm, gg_hbm)):
        wide[i] = full[i].astype(F32)
        copies.append(pltpu.make_async_copy(wide.at[i], dst, sem.at[1 + i]))
        copies[-1].start()

    def chunk(i):
        at = pl.ds(WIDE * i, WIDE)
        return at, pltpu.make_async_copy(grads.at[at], gf_hbm.at[at], sem.at[3 + i])

    def finish(i):
        at, copy = chunk(i)
        back = dot(dvalue[at].reshape(WIDE * TILE, D), wv[...], 1, 1).reshape(WIDE, TILE, D)
        grads[at] = (rest[at] + back).astype(BF16)
        copy.start()

    each(0, ROWS // WIDE, finish)
    each(0, ROWS // WIDE, lambda i: chunk(i)[1].wait())
    for copy in copies:
        copy.wait()


def per_device(
    features, w_value, w_gate, cotangent, local_rows, local_cols, local_count, local_tiles,
    remote_rows, remote_cols, remote_live, remote_tiles,
):
    hbm = pl.BlockSpec(memory_space=pl.ANY)
    vmem = pl.BlockSpec(memory_space=pltpu.VMEM)
    dma = pltpu.SemaphoreType.DMA
    blocks = (ROWS, TILE, D)
    tables = (local_rows, local_cols, remote_rows, remote_cols, remote_live)
    reduced = (2, NY, NX * NZ, 8, D)
    held = pl.pallas_call(
        kernel,
        name="relation",
        out_shape=(
            pltpu.VMEM(blocks, BF16),
            pltpu.VMEM(blocks, BF16),
            pltpu.VMEM(blocks, F32),
            pltpu.VMEM(reduced, BF16),
            pltpu.VMEM((D, D), BF16),
        ),
        in_specs=[pl.BlockSpec(memory_space=pltpu.SMEM)] + [hbm] * 11,
        out_specs=(vmem,) * 5,
        scratch_shapes=[
            *(pltpu.SMEM(a.shape, jnp.int32) for a in tables),
            pltpu.VMEM(blocks, BF16),
            pltpu.VMEM(blocks, BF16),
            pltpu.VMEM((D, D), BF16),
            pltpu.VMEM((LOC, TILE, TILE), BF16),
            pltpu.VMEM((NX * NZ, TILE, TILE), BF16),
            pltpu.VMEM((2, 3, 4, TILE, D), BF16),
            pltpu.VMEM((2, 2, 4, 4, TILE, D), BF16),
            pltpu.VMEM((2, 2, 4, 3, TILE, D), BF16),
            pltpu.VMEM((ZERO + 1, STEPS, TILE, D), F32),
            pltpu.VMEM(blocks, BF16),
            pltpu.VMEM(blocks, BF16),
            pltpu.VMEM((2, D, D), F32),
            pltpu.VMEM((D, D), F32),
            pltpu.VMEM((D, D), BF16),
            pltpu.VMEM((NY - 1, TILE, D), BF16),
            pltpu.VMEM((TILE, D), F32),
            pltpu.VMEM((NX * NZ, 8, D), BF16),
            pltpu.VMEM((PEERS, 8, D), BF16),
            pltpu.SMEM((6, LOC), jnp.int32),
            pltpu.SMEM((6, BLOCKS), jnp.int32),
            dma((11,)),
            dma((2, 2)),
            dma((2, 2, 3)),
            dma((2, 2, 4)),
            dma((2,)),
            dma((2,)),
            dma((2,)),
            dma((2,)),
            dma((2,)),
            dma((1 + PEERS // GROUP,)),
        ],
        compiler_params=pltpu.CompilerParams(
            collective_id=0, has_side_effects=True, vmem_limit_bytes=54000000
        ),
    )(
        local_count, *tables,
        features.reshape(blocks), cotangent.reshape(blocks), w_value, w_gate, local_tiles, remote_tiles,
    )
    wide = jax.ShapeDtypeStruct(reduced[1:], F32)
    out, grad, gv, gg = pl.pallas_call(
        emit,
        name="emit",
        out_shape=(jax.ShapeDtypeStruct(blocks, BF16), jax.ShapeDtypeStruct(blocks, BF16), wide, wide),
        in_specs=[vmem] * 5,
        out_specs=(hbm,) * 4,
        scratch_shapes=[pltpu.VMEM(blocks, BF16), pltpu.VMEM(reduced, F32), dma((3 + ROWS // WIDE,))],
        compiler_params=pltpu.CompilerParams(vmem_limit_bytes=16 << 20),
    )(*[pltpu.with_memory_space_constraint(a, pltpu.MemorySpace.VMEM) for a in held])
    return (
        out.reshape(features.shape),
        grad.reshape(features.shape),
        gv.reshape(D, D),
        gg.reshape(D, D),
    )


def solution(mesh):
    return jax.shard_map(
        per_device,
        mesh=mesh,
        in_specs=(
            P("tm", "asset", None),
            P(),
            P(),
            P("tm", "asset", None),
            P("asset"),
            P("asset"),
            P("asset"),
            P("asset", None, None),
            P("asset"),
            P("asset"),
            P("asset"),
            P("asset", None, None),
        ),
        out_specs=(P("tm", "asset", None), P("tm", "asset", None), P(), P()),
        check_vma=False,
    )
```

time: 117 us -> 109 us (0.932)
  Pallas kernels: 115 us -> 107 us
    pallas_call x1, Pallas kernels: 112 us -> 104 us  [per_device(): pl.pallas_call(kernel, name='relation', out_shape=(pltpu.VMEM(blocks, BF1...]
where the time goes in v3:
time: 109 us
  Pallas kernels  107 us (98%)
  between operations  1.29 us (1%)
    pallas_call x1, Pallas kernels, per_device(): pl.pallas_call(kernel, name='relation', out_shape=(pltpu.VMEM(blocks, BF1...  104 us
    pallas_call x1, Pallas kernels, per_device(): pl.pallas_call(emit, name='emit', out_shape=(jax.ShapeDtypeStruct(blocks,...  3.2 us

profile of v3, /device:TPU:1, one launch (start us, length us, event | category | flops | bytes accessed | tf_op | source)
XLA Modules:
  0.0 108.5 jit_solution(9395585025544260041)
XLA Ops:
  1.3 104.1 %relation.1 = (bf16[20,128,512]{2,1,0:T(8,128)(2,1)S(1)}, bf16[20,128,512]{2,1,0:T(8,128)(2,1)S(1)}, f32[20,128,512]{2,1,0:T(8,128)S(1)}, bf16[2,4,16,8,512]{4,3,2,1,0:T(8,128)(2,1)S(1)}, bf16[512,512]{1,0:T(8,128)(2,1)S(1)}) custom-call(s32[1]{0:T(128)S(6)} %copy.16.count, s32[20]{0:T(128)} %rows_hbm.1, s32[20]{0:T(128)} %cols_hbm.1, s32[16]{0:T(128)} %rrows_hbm.1, ...), custom_call_target="tpu_custom_call" | custom-call | tf_op jit(solution)/shard_map/relation/pallas_call | solution.py:460
  105.3 3.2 %emit.1 = (bf16[20,128,512]{2,1,0:T(8,128)(2,1)}, bf16[20,128,512]{2,1,0:T(8,128)(2,1)}, f32[4,16,8,512]{3,2,1,0:T(8,128)}, f32[4,16,8,512]{3,2,1,0:T(8,128)}) custom-call(bf16[20,128,512]{2,1,0:T(8,128)(2,1)S(1)} %get-tuple-element.13.outs, bf16[20,128,512]{2,1,0:T(8,128)(2,1)S(1)} %get-tuple-element.14.dvalue, f32[20,128,512]{2,1,0:T(8,128)S(1)} %get-tuple-element.15.rest, ...), custom_call_target="tpu_custom_call" | custom-call | tf_op jit(solution)/shard_map/emit/pallas_call | solution.py:513

commit v4 on v3

--- a/solution.py
+++ b/solution.py
@@ -87,11 +87,11 @@
 def kernel(
     count, rows_hbm, cols_hbm, rrows_hbm, rcols_hbm, rlive_hbm,
     feat_hbm, cot_hbm, wv_hbm, wg_hbm, lt_hbm, rt_hbm,
-    outs, gsum, gate, full, wv,
+    outs, gsum, gate, part, wv,
     rows, cols, rrows, rcols, rlive,
     feat, cot, wg, lt, rt,
     away, over, last, slots, dagg, dgate,
-    part, core_in, acc, y_in, mine, mine_out, xz_in,
+    full, core_in, acc, y_in, mine, mine_out, xz_in,
     links, heads,
     load_sem, ex_s, first_r, last_r,
     core_s, core_r, y_s, y_r, xz_s, xz_r,
@@ -249,6 +249,7 @@
         return dagg[h * BLOCKS + rrows[peer]]
 
     send(1, owed, lambda: None)
+    hand(1)
 
     def take_near(e, add):
         def direct(i):
@@ -355,7 +356,6 @@
         )
 
     each(0, PEERS, lambda k: spread(k).start())
-    hand(1)
     relay(1, 0, 2)
 
     def pre_step(i):
@@ -405,6 +405,10 @@
         device_id=core_peer(), device_id_type=MESH,
     )
     core_gather.start()
+    core_copy.wait_send()
+    core_gather.wait_recv()
+    for n in range(2):
+        part[n] = full[n].astype(F32).reshape(D, D)
     take_far(1, 4, 6, add_back)
 
     def settle(i):
@@ -414,21 +418,19 @@
     sent_away(1)
     for e in range(2):
         all_of(last.at[e], last.at[e], ex_s.at[e, 1], last_r.at[e, 0, 0]).wait_send()
-    core_copy.wait_send()
     y_all.wait_send()
     spread_all.wait_send()
     pieces = full.at[c, y, pl.ds(0, PEERS)]
     all_of(pieces, pieces, xz_s.at[1], xz_r.at[1]).wait_send()
     hand_all.wait_send()
-    core_gather.wait()
-
-
-def emit(outs, dvalue, rest, full, wv, out_hbm, gf_hbm, gv_hbm, gg_hbm, grads, wide, sem):
+    core_gather.wait_send()
+
+
+def emit(outs, dvalue, rest, part, wv, out_hbm, gf_hbm, gv_hbm, gg_hbm, grads, sem):
     copies = [pltpu.make_async_copy(outs, out_hbm, sem.at[0])]
     copies[0].start()
     for i, dst in enumerate((gv_hbm, gg_hbm)):
-        wide[i] = full[i].astype(F32)
-        copies.append(pltpu.make_async_copy(wide.at[i], dst, sem.at[1 + i]))
+        copies.append(pltpu.make_async_copy(part.at[i], dst, sem.at[1 + i]))
         copies[-1].start()
 
     def chunk(i):
@@ -464,7 +466,7 @@
             pltpu.VMEM(blocks, BF16),
             pltpu.VMEM(blocks, BF16),
             pltpu.VMEM(blocks, F32),
-            pltpu.VMEM(reduced, BF16),
+            pltpu.VMEM((2, D, D), F32),
             pltpu.VMEM((D, D), BF16),
         ),
         in_specs=[pl.BlockSpec(memory_space=pltpu.SMEM)] + [hbm] * 11,
@@ -482,7 +484,7 @@
             pltpu.VMEM((ZERO + 1, STEPS, TILE, D), F32),
             pltpu.VMEM(blocks, BF16),
             pltpu.VMEM(blocks, BF16),
-            pltpu.VMEM((2, D, D), F32),
+            pltpu.VMEM(reduced, BF16),
             pltpu.VMEM((D, D), F32),
             pltpu.VMEM((D, D), BF16),
             pltpu.VMEM((NY - 1, TILE, D), BF16),
@@ -503,27 +505,27 @@
             dma((1 + PEERS // GROUP,)),
         ],
         compiler_params=pltpu.CompilerParams(
-            collective_id=0, has_side_effects=True, vmem_limit_bytes=54000000
+            collective_id=0, has_side_effects=True, vmem_limit_bytes=53000000
         ),
     )(
         local_count, *tables,
         features.reshape(blocks), cotangent.reshape(blocks), w_value, w_gate, local_tiles, remote_tiles,
     )
-    wide = jax.ShapeDtypeStruct(reduced[1:], F32)
+    square = jax.ShapeDtypeStruct((D, D), F32)
     out, grad, gv, gg = pl.pallas_call(
         emit,
         name="emit",
-        out_shape=(jax.ShapeDtypeStruct(blocks, BF16), jax.ShapeDtypeStruct(blocks, BF16), wide, wide),
+        out_shape=(jax.ShapeDtypeStruct(blocks, BF16), jax.ShapeDtypeStruct(blocks, BF16), square, square),
         in_specs=[vmem] * 5,
         out_specs=(hbm,) * 4,
-        scratch_shapes=[pltpu.VMEM(blocks, BF16), pltpu.VMEM(reduced, F32), dma((3 + ROWS // WIDE,))],
+        scratch_shapes=[pltpu.VMEM(blocks, BF16), dma((3 + ROWS // WIDE,))],
         compiler_params=pltpu.CompilerParams(vmem_limit_bytes=16 << 20),
     )(*[pltpu.with_memory_space_constraint(a, pltpu.MemorySpace.VMEM) for a in held])
     return (
         out.reshape(features.shape),
         grad.reshape(features.shape),
-        gv.reshape(D, D),
-        gg.reshape(D, D),
+        gv,
+        gg,
     )
 
 

time: 109 us -> 108 us (level)
  no operation moved by 1% of the time
where the time goes in v4:
time: 108 us
  Pallas kernels  107 us (99%)
  between operations  1.29 us (1%)
    pallas_call x1, Pallas kernels, per_device(): pl.pallas_call(kernel, name='relation', out_shape=(pltpu.VMEM(blocks, BF1...  103 us
    pallas_call x1, Pallas kernels, per_device(): pl.pallas_call(emit, name='emit', out_shape=(jax.ShapeDtypeStruct(blocks,...  3.06 us

profile of v4, /device:TPU:1, one launch (start us, length us, event | category | flops | bytes accessed | tf_op | source)
XLA Modules:
  0.0 107.8 jit_solution(15364271117558258575)
XLA Ops:
  1.3 103.5 %relation.1 = (bf16[20,128,512]{2,1,0:T(8,128)(2,1)S(1)}, bf16[20,128,512]{2,1,0:T(8,128)(2,1)S(1)}, f32[20,128,512]{2,1,0:T(8,128)S(1)}, f32[2,512,512]{2,1,0:T(8,128)S(1)}, bf16[512,512]{1,0:T(8,128)(2,1)S(1)}) custom-call(s32[1]{0:T(128)S(6)} %copy.16.count, s32[20]{0:T(128)} %rows_hbm.1, s32[20]{0:T(128)} %cols_hbm.1, s32[16]{0:T(128)} %rrows_hbm.1, ...), custom_call_target="tpu_custom_call" | custom-call | tf_op jit(solution)/shard_map/relation/pallas_call | solution.py:462
  104.8 3.1 %emit.1 = (bf16[20,128,512]{2,1,0:T(8,128)(2,1)}, bf16[20,128,512]{2,1,0:T(8,128)(2,1)}, f32[512,512]{1,0:T(8,128)}, f32[512,512]{1,0:T(8,128)}) custom-call(bf16[20,128,512]{2,1,0:T(8,128)(2,1)S(1)} %get-tuple-element.13.outs, bf16[20,128,512]{2,1,0:T(8,128)(2,1)S(1)} %get-tuple-element.14.dvalue, f32[20,128,512]{2,1,0:T(8,128)S(1)} %get-tuple-element.15.rest, ...), custom_call_target="tpu_custom_call" | custom-call | tf_op jit(solution)/shard_map/emit/pallas_call | solution.py:515

commit v5 on v4

--- a/solution.py
+++ b/solution.py
@@ -115,9 +115,9 @@
             (wv_hbm, wv),
         )
     ):
-        copy = pltpu.make_async_copy(src, dst, load_sem.at[i])
+        loads.append(pltpu.make_async_copy(src, dst, load_sem.at[i]))
+    for copy in loads[:4]:
         copy.start()
-        loads.append(copy)
 
     def core_peer():
         return (y * NC + (1 - c), asset)
@@ -200,6 +200,8 @@
 
     for copy in loads[:4]:
         copy.wait()
+    for copy in loads[4:]:
+        copy.start()
 
     def term(h, peer):
         return dot(masked(peer), feat[h * BLOCKS + rcols[peer]], 1, 0).astype(BF16)

time: 108 us -> 108 us (level)
  no operation moved by 1% of the time
where the time goes in v5:
time: 108 us
  Pallas kernels  107 us (99%)
  between operations  1.29 us (1%)
    pallas_call x1, Pallas kernels, per_device(): pl.pallas_call(kernel, name='relation', out_shape=(pltpu.VMEM(blocks, BF1...  103 us
    pallas_call x1, Pallas kernels, per_device(): pl.pallas_call(emit, name='emit', out_shape=(jax.ShapeDtypeStruct(blocks,...  3.06 us

profile of v5, /device:TPU:1, one launch (start us, length us, event | category | flops | bytes accessed | tf_op | source)
XLA Modules:
  0.0 107.8 jit_solution(6160727179941022710)
XLA Ops:
  1.3 103.5 %relation.1 = (bf16[20,128,512]{2,1,0:T(8,128)(2,1)S(1)}, bf16[20,128,512]{2,1,0:T(8,128)(2,1)S(1)}, f32[20,128,512]{2,1,0:T(8,128)S(1)}, f32[2,512,512]{2,1,0:T(8,128)S(1)}, bf16[512,512]{1,0:T(8,128)(2,1)S(1)}) custom-call(s32[1]{0:T(128)S(6)} %copy.16.count, s32[20]{0:T(128)} %rows_hbm.1, s32[20]{0:T(128)} %cols_hbm.1, s32[16]{0:T(128)} %rrows_hbm.1, ...), custom_call_target="tpu_custom_call" | custom-call | tf_op jit(solution)/shard_map/relation/pallas_call | solution.py:464
  104.8 3.1 %emit.1 = (bf16[20,128,512]{2,1,0:T(8,128)(2,1)}, bf16[20,128,512]{2,1,0:T(8,128)(2,1)}, f32[512,512]{1,0:T(8,128)}, f32[512,512]{1,0:T(8,128)}) custom-call(bf16[20,128,512]{2,1,0:T(8,128)(2,1)S(1)} %get-tuple-element.13.outs, bf16[20,128,512]{2,1,0:T(8,128)(2,1)S(1)} %get-tuple-element.14.dvalue, f32[20,128,512]{2,1,0:T(8,128)S(1)} %get-tuple-element.15.rest, ...), custom_call_target="tpu_custom_call" | custom-call | tf_op jit(solution)/shard_map/emit/pallas_call | solution.py:517
